TPU v7x, 32 devices: a whole 2x2x4 slice. The times are simulated.
32 devices in a mesh: dp: 16 (over z, y, core), tensor: 2 (over x).
Axes of the slice: x: 2, y: 2, z: 4, core: 2. Of those that a mesh axis runs over, the one named last changes fastest.
Arguments:
- x_in: bfloat16 [32768, 768], P(('dp', 'tensor')), may hold values from -6 to 6
- lengths: int32 [32], P('dp'), may hold values from 256 to 1024, as said below
- cotangent: bfloat16 [32768, 768], P(('dp', 'tensor')), may hold values from -6 to 6
- w_query: bfloat16 [768, 768], P('dp', 'tensor'), may hold values from -0.5 to 0.5
- w_key: bfloat16 [768, 768], P('dp', 'tensor'), may hold values from -0.5 to 0.5
- w_value: bfloat16 [768, 768], P('dp', 'tensor'), may hold values from -0.21875 to 0.21875
- w_out: bfloat16 [768, 768], P('tensor', 'dp'), may hold values from -0.21875 to 0.21875
- w_in: bfloat16 [768, 3072], P('dp', 'tensor'), may hold values from -0.21875 to 0.21875
- w_down: bfloat16 [3072, 768], P('tensor', 'dp'), may hold values from -0.109375 to 0.109375
- conv_weight: float32 [12, 33], P('tensor'), may hold values from -1 to 1
- ln1_gain: float32 [768], P(('dp', 'tensor')), may hold values from 0.5 to 1.5
- ln1_bias: float32 [768], P(('dp', 'tensor')), may hold values from -1.8 to 1.8
- ln2_gain: float32 [768], P(('dp', 'tensor')), may hold values from 0.5 to 1.5
- ln2_bias: float32 [768], P(('dp', 'tensor')), may hold values from -1.8 to 1.8
Outputs:
- output: bfloat16 [32768, 768], P(('dp', 'tensor'))
- input_grad: bfloat16 [32768, 768], P(('dp', 'tensor'))
- grad_query: float32 [768, 768], P('dp', 'tensor')
- grad_key: float32 [768, 768], P('dp', 'tensor')
- grad_value: float32 [768, 768], P('dp', 'tensor')
- grad_out: float32 [768, 768], P('tensor', 'dp')
- grad_in: float32 [768, 3072], P('dp', 'tensor')
- grad_down: float32 [3072, 768], P('tensor', 'dp')
- grad_conv: float32 [12, 33], P('tensor')
- grad_ln1_gain: float32 [768], P(('dp', 'tensor'))
- grad_ln1_bias: float32 [768], P(('dp', 'tensor'))
- grad_ln2_gain: float32 [768], P(('dp', 'tensor'))
- grad_ln2_bias: float32 [768], P(('dp', 'tensor'))
- stats: float32 [3], replicated
Inputs may be any that keep to these rules, and one draw needn't show every extreme that they name: `lengths`: the valid tokens of a sequence are its first ones; in every draw some sequence fills all 1024 slots.
All inputs are finite; a program needn't handle non-finite values.
Results may differ from a plain program's by a relative error of at most 0.017.
Values may be sent and summed in bfloat16 or wider, within the bound.
A program may use at most 320 MiB of HBM per device.

v0:
```python
from functools import partial

import jax
import jax.numpy as jnp
from jax import lax
from jax.sharding import PartitionSpec as P

D = 768
HEADS = 12
LANDMARKS = 64
PINV_STEPS = 6


def exact_einsum_product(formula, left_op, right_op):
    return jnp.einsum(formula, left_op, right_op, precision=lax.Precision.HIGHEST)


def layer_norm(values, gain_vec, shift_vec):
    centre = values - jnp.mean(values, axis=-1, keepdims=True)
    spread = jnp.mean(centre * centre, axis=-1, keepdims=True)
    return centre * lax.rsqrt(spread + 1e-05) * gain_vec + shift_vec


def iterative_pseudo_inverse(matrix):
    identity_mat = jnp.eye(matrix.shape[-1], dtype=matrix.dtype)
    column_sums = jnp.sum(matrix, axis=-2)
    largest = jnp.max(column_sums, axis=-1)
    inverse = jnp.swapaxes(matrix, -1, -2) / largest[:, None, None]
    for sweep_no in range(PINV_STEPS):
        product = exact_einsum_product("hij,hjk->hik", matrix, inverse)
        inner_term = 7.0 * identity_mat - product
        inner_term = 15.0 * identity_mat - exact_einsum_product("hij,hjk->hik", product, inner_term)
        inner_term = 13.0 * identity_mat - exact_einsum_product("hij,hjk->hik", product, inner_term)
        inverse = exact_einsum_product("hij,hjk->hik", 0.25 * inverse, inner_term)
    return inverse


def nystrom(queries, keys_in, values_in, valid_mask, conv_taps):
    length = queries.shape[0]
    head_count = conv_taps.shape[0]
    head_width = queries.shape[1] // head_count
    scale_factor = head_width ** (-0.25)

    def split_heads(tensor):
        return tensor.reshape(length, head_count, head_width).transpose(1, 0, 2)

    query_heads = split_heads(queries * valid_mask[:, None] * scale_factor)
    key_heads = split_heads(keys_in * valid_mask[:, None] * scale_factor)
    value_heads = split_heads(values_in * valid_mask[:, None])
    query_landmark_rows = jnp.mean(
        query_heads.reshape(head_count, LANDMARKS, length // LANDMARKS, head_width), axis=2
    )
    key_landmark_rows = jnp.mean(
        key_heads.reshape(head_count, LANDMARKS, length // LANDMARKS, head_width), axis=2
    )
    kernel_one = jax.nn.softmax(
        exact_einsum_product("hsd,hld->hsl", query_heads, key_landmark_rows), axis=-1
    )
    landmark_kernel_matrix = jax.nn.softmax(
        exact_einsum_product("sux,sgx->sug", query_landmark_rows, key_landmark_rows), axis=-1
    )
    scores = exact_einsum_product("hld,hsd->hls", query_landmark_rows, key_heads)
    scores = jnp.where(valid_mask[None, None, :] > 0.5, scores, -1000000000.0)
    kernel_three = jax.nn.softmax(scores, axis=-1)
    result_overview = exact_einsum_product("hls,hsd->hld", kernel_three, value_heads)
    result_overview = exact_einsum_product(
        "fba,fau->fbu", iterative_pseudo_inverse(landmark_kernel_matrix), result_overview
    )
    mixture = exact_einsum_product("hsl,hld->hsd", kernel_one, result_overview)
    half_taps = conv_taps.shape[1] // 2
    padded = jnp.pad(value_heads, ((0, 0), (half_taps, half_taps), (0, 0)))
    for offset in range(conv_taps.shape[1]):
        mixture = (
            mixture + conv_taps[:, offset, None, None] * padded[:, offset : offset + length, :]
        )
    return mixture.transpose(1, 0, 2).reshape(length, head_count * head_width)


def contract_rows(left_op, right_op):
    return lax.dot_general(
        left_op, right_op, (((0,), (0,)), ((), ())), preferred_element_type=jnp.float32
    )


def contracted_columns(left_op, right_op):
    return lax.dot_general(
        left_op, right_op, (((1,), (1,)), ((), ())), preferred_element_type=jnp.float32
    )


def per_device(
    x_in,
    lengths,
    cotangent,
    w_query,
    w_key,
    w_value,
    w_out,
    w_in,
    w_down,
    conv_weight,
    ln1_gain,
    ln1_bias,
    ln2_gain,
    ln2_bias,
):
    tensor_index = lax.axis_index("tensor")
    row_count = x_in.shape[0]
    seq_count = lengths.shape[0]
    slot_len = row_count * lax.axis_size("tensor") // seq_count
    positions = jnp.arange(slot_len, dtype=jnp.int32)
    seq_mask = (positions[None, :] < lengths[:, None]).astype(jnp.float32)
    local_mask = lax.dynamic_slice_in_dim(seq_mask.reshape(-1), tensor_index * row_count, row_count)
    gathered = (
        lax.all_gather(w_query, "dp", axis=0, tiled=True),
        lax.all_gather(w_key, "dp", axis=0, tiled=True),
        lax.all_gather(w_value, "dp", axis=0, tiled=True),
        lax.all_gather(w_out, "dp", axis=1, tiled=True),
        lax.all_gather(w_in, "dp", axis=0, tiled=True),
        lax.all_gather(w_down, "dp", axis=1, tiled=True),
    )
    query_full, key_full, value_full, out_full, in_full, down_full = gathered
    gain_one, bias_one, gain_two, bias_two = (
        lax.all_gather(ln1_gain, ("dp", "tensor"), axis=0, tiled=True),
        lax.all_gather(ln1_bias, ("dp", "tensor"), axis=0, tiled=True),
        lax.all_gather(ln2_gain, ("dp", "tensor"), axis=0, tiled=True),
        lax.all_gather(ln2_bias, ("dp", "tensor"), axis=0, tiled=True),
    )
    tokens_all = lax.all_gather(x_in, "tensor", axis=0, tiled=True)
    queries = jnp.dot(tokens_all, query_full, preferred_element_type=jnp.float32)
    keys_all = jnp.dot(tokens_all, key_full, preferred_element_type=jnp.float32)
    values_all = jnp.dot(tokens_all, value_full, preferred_element_type=jnp.float32)
    local_width = queries.shape[1]

    def attend(query_arg, key_arg, value_arg, conv_taps):
        shaped = (seq_count, slot_len, local_width)
        result = jax.vmap(nystrom, in_axes=(0, 0, 0, 0, None))(
            query_arg.reshape(shaped),
            key_arg.reshape(shaped),
            value_arg.reshape(shaped),
            seq_mask,
            conv_taps,
        )
        return result.reshape(seq_count * slot_len, local_width)

    context, attend_back = jax.vjp(attend, queries, keys_all, values_all, conv_weight)
    context_low = context.astype(jnp.bfloat16)
    attn_branch = lax.psum_scatter(
        jnp.dot(context_low, out_full, preferred_element_type=jnp.float32).astype(jnp.bfloat16),
        "tensor",
        scatter_dimension=0,
        tiled=True,
    ).astype(jnp.float32)
    tokens_local = x_in.astype(jnp.float32)
    hidden_f, norm_one_back = jax.vjp(layer_norm, tokens_local + attn_branch, gain_one, bias_one)
    hidden_low = hidden_f.astype(jnp.bfloat16)
    hidden_all = lax.all_gather(hidden_low, "tensor", axis=0, tiled=True)
    pre_act = jnp.dot(hidden_all, in_full, preferred_element_type=jnp.float32)
    act_f, gelu_back = jax.vjp(partial(jax.nn.gelu, approximate=False), pre_act)
    act_low = act_f.astype(jnp.bfloat16)
    ffn_branch = lax.psum_scatter(
        jnp.dot(act_low, down_full, preferred_element_type=jnp.float32).astype(jnp.bfloat16),
        "tensor",
        scatter_dimension=0,
        tiled=True,
    ).astype(jnp.float32)
    output_f, norm_two_back = jax.vjp(
        layer_norm, hidden_low.astype(jnp.float32) + ffn_branch, gain_two, bias_two
    )
    output = output_f.astype(jnp.bfloat16)
    grad_result = cotangent.astype(jnp.float32) * local_mask[:, None]
    grad_resid_two, grad_gain_two, grad_bias_two = norm_two_back(grad_result)
    grad_branch_all = lax.all_gather(
        grad_resid_two.astype(jnp.bfloat16), "tensor", axis=0, tiled=True
    )
    back_weights = (
        lax.all_gather(w_query, "dp", axis=0, tiled=True),
        lax.all_gather(w_key, "dp", axis=0, tiled=True),
        lax.all_gather(w_value, "dp", axis=0, tiled=True),
        lax.all_gather(w_out, "dp", axis=1, tiled=True),
        lax.all_gather(w_in, "dp", axis=0, tiled=True),
        lax.all_gather(w_down, "dp", axis=1, tiled=True),
    )
    query_back, key_back, value_back, out_back, in_back, down_back = back_weights
    grad_act = contracted_columns(grad_branch_all, down_back)
    grad_down_full = contract_rows(act_low, grad_branch_all)
    grad_pre = gelu_back(grad_act)[0].astype(jnp.bfloat16)
    grad_in_full = contract_rows(hidden_all, grad_pre)
    grad_hidden = lax.psum_scatter(
        contracted_columns(grad_pre, in_back).astype(jnp.bfloat16),
        "tensor",
        scatter_dimension=0,
        tiled=True,
    ).astype(jnp.float32)
    grad_resid_one, grad_gain_one, grad_bias_one = norm_one_back(grad_hidden + grad_resid_two)
    grad_attn_all = lax.all_gather(
        grad_resid_one.astype(jnp.bfloat16), "tensor", axis=0, tiled=True
    )
    grad_context = contracted_columns(grad_attn_all, out_back)
    grad_out_full = contract_rows(context_low, grad_attn_all)
    grad_query_f, grad_key_f, grad_value_f, grad_conv_local = attend_back(grad_context)
    grad_query_low = grad_query_f.astype(jnp.bfloat16)
    grad_key_low = grad_key_f.astype(jnp.bfloat16)
    value_gradient_reduced = grad_value_f.astype(jnp.bfloat16)
    input_part = (
        contracted_columns(grad_query_low, query_back)
        + contracted_columns(grad_key_low, key_back)
        + contracted_columns(value_gradient_reduced, value_back)
    )
    grad_tokens = lax.psum_scatter(
        input_part.astype(jnp.bfloat16), "tensor", scatter_dimension=0, tiled=True
    ).astype(jnp.float32)
    input_grad = (grad_resid_one + grad_tokens).astype(jnp.bfloat16)
    grad_query_full = contract_rows(tokens_all, grad_query_low)
    grad_key_full = contract_rows(tokens_all, grad_key_low)
    grad_value_full = contract_rows(tokens_all, value_gradient_reduced)
    weight_grads = (
        lax.psum_scatter(grad_query_full, "dp", scatter_dimension=0, tiled=True),
        lax.psum_scatter(grad_key_full, "dp", scatter_dimension=0, tiled=True),
        lax.psum_scatter(grad_value_full, "dp", scatter_dimension=0, tiled=True),
        lax.psum_scatter(grad_out_full, "dp", scatter_dimension=1, tiled=True),
        lax.psum_scatter(grad_in_full, "dp", scatter_dimension=0, tiled=True),
        lax.psum_scatter(grad_down_full, "dp", scatter_dimension=1, tiled=True),
    )
    head_local = conv_weight.shape[0]
    conv_full = lax.dynamic_update_slice_in_dim(
        jnp.zeros((HEADS, conv_weight.shape[1]), jnp.float32),
        grad_conv_local,
        tensor_index * head_local,
        0,
    )
    stat_terms = jnp.stack(
        [
            jnp.sum(local_mask[:, None] * tokens_local * tokens_local),
            jnp.sum(local_mask[:, None] * attn_branch * attn_branch),
            jnp.sum(local_mask[:, None] * ffn_branch * ffn_branch),
            jnp.sum(local_mask),
        ]
    )
    summed = lax.psum(
        (grad_gain_one, grad_bias_one, grad_gain_two, grad_bias_two, conv_full, stat_terms),
        ("dp", "tensor"),
    )
    share = D // lax.axis_size(("dp", "tensor"))
    start_at = lax.axis_index(("dp", "tensor")) * share

    def take_share(vector):
        return lax.dynamic_slice_in_dim(vector, start_at, share)

    conv_grad = lax.dynamic_slice_in_dim(summed[4], tensor_index * head_local, head_local, 0)
    stat_sums = summed[5]
    stats = jnp.sqrt(stat_sums[:3] / (stat_sums[3] * D))
    return (
        output,
        input_grad,
        weight_grads[0],
        weight_grads[1],
        weight_grads[2],
        weight_grads[3],
        weight_grads[4],
        weight_grads[5],
        conv_grad,
        take_share(summed[0]),
        take_share(summed[1]),
        take_share(summed[2]),
        take_share(summed[3]),
        stats,
    )


def solution(mesh):
    in_specs = (
        P(("dp", "tensor"), None),
        P("dp"),
        P(("dp", "tensor"), None),
        P("dp", "tensor"),
        P("dp", "tensor"),
        P("dp", "tensor"),
        P("tensor", "dp"),
        P("dp", "tensor"),
        P("tensor", "dp"),
        P("tensor", None),
        P(("dp", "tensor")),
        P(("dp", "tensor")),
        P(("dp", "tensor")),
        P(("dp", "tensor")),
    )
    out_specs = (
        P(("dp", "tensor"), None),
        P(("dp", "tensor"), None),
        P("dp", "tensor"),
        P("dp", "tensor"),
        P("dp", "tensor"),
        P("tensor", "dp"),
        P("dp", "tensor"),
        P("tensor", "dp"),
        P("tensor", None),
        P(("dp", "tensor")),
        P(("dp", "tensor")),
        P(("dp", "tensor")),
        P(("dp", "tensor")),
        P(),
    )
    return jax.shard_map(
        per_device, mesh=mesh, in_specs=in_specs, out_specs=out_specs, check_vma=False
    )
```

profile of v0, /device:TPU:0, one launch (start us, length us, event | category | flops | bytes accessed | tf_op | source)
XLA Modules:
  0.0 1302.5 jit_solution(2519137076501570210)
XLA Ops:
  15.4 26.5 %all_gather.49 = bf16[768,384]{1,0:T(8,128)(2,1)} all-gather(bf16[48,384]{1,0:T(8,128)(2,1)} %param.17), channel_id=1, replica_groups=mesh['dp'=16,'tensor'=2] {'dp'}, dimensions={0}, use_global_device_ids=true | all-gather | bytes 626688 | tf_op jit(solution)/shard_map/all_gather | solution.py:115
  41.9 20.7 %all_gather.50 = bf16[768,384]{1,0:T(8,128)(2,1)} all-gather(bf16[48,384]{1,0:T(8,128)(2,1)} %param.18), channel_id=1, replica_groups=mesh['dp'=16,'tensor'=2] {'dp'}, dimensions={0}, use_global_device_ids=true | all-gather | bytes 626688 | tf_op jit(solution)/shard_map/all_gather | solution.py:116
  62.6 22.2 %all_gather.51 = bf16[768,384]{1,0:T(8,128)(2,1)} all-gather(bf16[48,384]{1,0:T(8,128)(2,1)} %param.19), channel_id=1, replica_groups=mesh['dp'=16,'tensor'=2] {'dp'}, dimensions={0}, use_global_device_ids=true | all-gather | bytes 626688 | tf_op jit(solution)/shard_map/all_gather | solution.py:117
  84.8 20.4 %all_gather.52 = bf16[384,768]{0,1:T(8,128)(2,1)} all-gather(bf16[384,48]{0,1:T(8,128)(2,1)S(1)} %copy-done.152), channel_id=1, replica_groups=mesh['dp'=16,'tensor'=2] {'dp'}, dimensions={1}, use_global_device_ids=true | all-gather | bytes 626688 | tf_op jit(solution)/shard_map/all_gather | solution.py:118
  195.8 28.8 %fusion.61 = bf16[2,1024,6,64]{1,3,2,0:T(8,128)(2,1)S(1)} fusion(f32[2,6,1024,64]{2,3,1,0:T(8,128)S(1)} %get-tuple-element.185, f32[6]{0:T(128)S(1)} %copy-done.170, f32[6]{0:T(128)S(1)} %copy-done.172, f32[6]{0:T(128)S(1)} %copy-done.174, f32[6]{0:T(128)S(1)} %copy-done.205, f32[6]{0:T(128)S(1)} %copy-done.210, f32[6]{0:T(128)S(1)} %copy-done.212, ...), kind=kOutput, calls=%fused_computation.221 | convolution fusion | flops 657457152 | bytes 8110872 | tf_op jit(solution)/shard_map/jvp(vmap(hsl,hld->hsd))/dot_general | solution.py:15
  232.8 40.3 %all-reduce.72 = (f32[768]{0:T(1024)S(1)}, f32[768]{0:T(1024)S(1)}, f32[768]{0:T(1024)S(1)}) all-reduce(f32[768]{0:T(1024)S(1)} %dynamic-update-slice.1, f32[768]{0:T(1024)S(1)} %dynamic-update-slice, f32[768]{0:T(1024)S(1)} %dynamic-update-slice.2), channel_id=1, replica_groups=mesh['dp'=16,'tensor'=2] {'dp','tensor'}, use_global_device_ids=true, to_apply=%add.68 | all-reduce | flops 2304 | bytes 18432
  281.7 43.8 %all-gather.9.cloned.1.call-done = bf16[2048,768]{1,0:T(8,128)(2,1)} async-done(((bf16[1024,768]{1,0:T(8,128)(2,1)}), bf16[2048,768]{1,0:T(8,128)(2,1)}) %all-gather.9.cloned.1.call-update) | async-done | bytes 3145744 | tf_op jit(solution)/shard_map/all_gather | solution.py:157
  325.5 34.3 %multiply_convert_fusion = (bf16[2048,1536]{1,0:T(8,128)(2,1)}, f32[2048,1536]{1,0:T(8,128)}, f32[2048,1536]{1,0:T(8,128)}) fusion(bf16[2048,768]{1,0:T(8,128)(2,1)} %all-gather.9.cloned.1.call-done, bf16[768,1536]{1,0:T(8,128)(2,1)} %all-gather.11.cloned.1.call-done), kind=kOutput, calls=%fused_computation.5 | convolution fusion | flops 5036310528 | bytes 36962304 | tf_op jit(solution)/shard_map/dot_general | solution.py:158
  380.8 40.5 %reduce-scatter.19.cloned.1.call-done = bf16[1024,768]{1,0:T(8,128)(2,1)} async-done(((bf16[2048,768]{1,0:T(8,128)(2,1)}), bf16[1024,768]{1,0:T(8,128)(2,1)}) %reduce-scatter.19.cloned.1.call-update) | async-done | bytes 1572880 | tf_op jit(solution)/shard_map/reduce_scatter | solution.py:161
  432.9 44.6 %all-gather.15.cloned.1.call-done = bf16[2048,768]{1,0:T(8,128)(2,1)} async-done(((bf16[1024,768]{1,0:T(8,128)(2,1)}), bf16[2048,768]{1,0:T(8,128)(2,1)}) %all-gather.15.cloned.1.call-update) | async-done | bytes 3145744 | tf_op jit(solution)/shard_map/all_gather | solution.py:173
  477.6 14.2 %add_convert_fusion = bf16[2048,1536]{1,0:T(8,128)(2,1)S(1)} fusion(f32[2048,1536]{1,0:T(8,128)} %get-tuple-element.150, f32[2048,1536]{1,0:T(8,128)} %get-tuple-element.195, bf16[2048,768]{1,0:T(8,128)(2,1)} %all-gather.15.cloned.1.call-done, bf16[1536,768]{0,1:T(8,128)(2,1)S(1)} %copy-done.236), kind=kOutput, calls=%fused_computation.4 | convolution fusion | flops 4875878400 | bytes 36962304 | tf_op jit(solution)/shard_map/dot_general | solution.py:86
  500.9 43.4 %reduce-scatter.21.cloned.1.call-done = bf16[1024,768]{1,0:T(8,128)(2,1)} async-done(((bf16[2048,768]{1,0:T(8,128)(2,1)}), bf16[1024,768]{1,0:T(8,128)(2,1)}) %reduce-scatter.21.cloned.1.call-update) | async-done | bytes 1572880 | tf_op jit(solution)/shard_map/reduce_scatter | solution.py:189
  559.1 41.3 %all-gather.17.cloned.1.call-done = bf16[2048,768]{1,0:T(8,128)(2,1)} async-done(((bf16[1024,768]{1,0:T(8,128)(2,1)}), bf16[2048,768]{1,0:T(8,128)(2,1)}) %all-gather.17.cloned.1.call-update) | async-done | bytes 3145744 | tf_op jit(solution)/shard_map/all_gather | solution.py:196
  652.9 15.1 %fusion.18 = (f32[6]{0:T(128)}, f32[6]{0:T(128)}, f32[6]{0:T(128)}, f32[6]{0:T(128)}, f32[6]{0:T(128)}, /*index=5*/f32[6]{0:T(128)}, f32[6]{0:T(128)}, f32[6]{0:...) fusion(f32[2,6,1024,64]{2,3,1,0:T(8,128)S(1)} %copy-done.9, ...), kind=kLoop, calls=%fused_computation.115 | loop fusion | flops 25952166 | bytes 15729072 | tf_op jit(solution)/shard_map/transpose(jvp(vmap()))/reduce_sum | solution.py:74
  668.1 14.7 %bitcast_multiply_fusion.61 = (f32[2,6,1024,64]{2,3,1,0:T(8,128)}, f32[2,6,1024,64]{2,3,1,0:T(8,128)}, f32[2,6,1024,64]{2,3,1,0:T(8,128)}, f32[2,6,1024,64]{2,3,...) fusion(f32[6]{0:T(128)S(1)} %copy-done.211, ...), kind=kLoop, calls=%fused_computation.105 | loop fusion | flops 9437184 | bytes 40894752 | tf_op jit(solution)/shard_map/transpose(jvp(vmap()))/mul | solution.py:74
  682.8 22.6 %bitcast_multiply_fusion.62 = (f32[2,6,1024,64]{2,3,1,0:T(8,128)}, f32[2,6,1024,64]{2,3,1,0:T(8,128)}, f32[2,6,1024,64]{2,3,1,0:T(8,128)}, f32[2,6,1024,64]{2,3,...) fusion(f32[6]{0:T(128)} %get-tuple-element.100, ...), kind=kLoop, calls=%fused_computation.106 | loop fusion | flops 14155776 | bytes 59769264 | tf_op jit(solution)/shard_map/transpose(jvp(vmap()))/mul | solution.py:74
  789.1 35.1 %pad_add_fusion = f32[2,6,1056,64]{2,3,1,0:T(8,128)} fusion(f32[2,6,1024,64]{2,3,1,0:T(8,128)} %get-tuple-element.161, f32[2,6,1024,64]{2,3,1,0:T(8,128)} %get-tuple-element.162, f32[2,6,1024,64]{2,3,1,0:T(8,128)} %get-tuple-element.163, f32[2,6,1024,64]{2,3,1,0:T(8,128)} %get-tuple-element.164, f32[2,6,1024,64]{2,3,1,0:T(8,128)} %get-tuple-element.165, ...), kind=kLoop, calls=%fused_computation.29 | loop fusion | flops 21086208 | bytes 88178688 | tf_op jit(solution)/shard_map/transpose(jvp(vmap()))/add_any | solution.py:74
  898.7 37.2 %fusion.17 = (f32[6]{0:T(128)S(1)}, f32[6]{0:T(128)S(1)}, f32[6]{0:T(128)S(1)}, f32[6]{0:T(128)S(1)}, f32[6]{0:T(128)S(1)}, /*index=5*/f32[6]{0:T(128)S(1)}, f32...) fusion(f32[2,6,1024,64]{2,3,1,0:T(8,128)} %copy-done.8, ...), kind=kLoop, calls=%fused_computation.114 | loop fusion | flops 28311444 | bytes 6291888 | tf_op jit(solution)/shard_map/transpose(jvp(vmap()))/reduce_sum | solution.py:74
  936.3 40.9 %all-reduce.71 = (f32[768]{0:T(1024)S(1)}, f32[12,33]{1,0:T(8,128)S(1)}, f32[768]{0:T(1024)S(1)}, f32[768]{0:T(1024)S(1)}, f32[768]{0:T(1024)S(1)}, /*index=5*/f32[768]{0:T(1024)S(1)}, f32[4]{0:T(128)S(1)}) all-reduce(f32[768]{0:T(1024)S(1)} %dynamic-update-slice.3, ...), channel_id=1, replica_groups=mesh['dp'=16,'tensor'=2] {'dp','tensor'}, use_global_device_ids=true, to_apply=%add.70 | all-reduce | flops 4240 | bytes 33920
  989.0 60.0 %reduce-scatter.27.cloned.1.call-done = f32[48,1536]{1,0:T(8,128)} async-done(((f32[768,1536]{1,0:T(8,128)}), f32[48,1536]{1,0:T(8,128)}) %reduce-scatter.27.cloned.1.call-update) | async-done | bytes 294928 | tf_op jit(solution)/shard_map/reduce_scatter | solution.py:222
  1049.0 61.5 %reduce-scatter.25.cloned.1.call-done = f32[384,48]{0,1:T(8,128)} async-done(((f32[384,768]{0,1:T(8,128)}), f32[384,48]{0,1:T(8,128)}) %reduce-scatter.25.cloned.1.call-update) | async-done | bytes 73744 | tf_op jit(solution)/shard_map/reduce_scatter | solution.py:221
  1110.6 61.4 %reduce-scatter.31.cloned.1.call-done = f32[48,384]{1,0:T(8,128)} async-done(((f32[768,384]{1,0:T(8,128)}), f32[48,384]{1,0:T(8,128)}) %reduce-scatter.31.cloned.1.call-update) | async-done | bytes 73744
  1172.0 61.3 %reduce-scatter.33.cloned.1.call-done = f32[48,384]{1,0:T(8,128)} async-done(((f32[768,384]{1,0:T(8,128)}), f32[48,384]{1,0:T(8,128)}) %reduce-scatter.33.cloned.1.call-update) | async-done | bytes 73744
  1233.3 61.4 %reduce-scatter.35.cloned.1.call-done = f32[48,384]{1,0:T(8,128)} async-done(((f32[768,384]{1,0:T(8,128)}), f32[48,384]{1,0:T(8,128)}) %reduce-scatter.35.cloned.1.call-update) | async-done | bytes 73744
  (716 shorter events, 389.4 us)
Async XLA Ops:
  8.0 76.8 %copy-start.152 = (bf16[384,48]{0,1:T(8,128)(2,1)S(1)}, bf16[384,48]{0,1:T(8,128)(2,1)}, u32[]{:S(2)}) copy-start(bf16[384,48]{0,1:T(8,128)(2,1)} %param.20) | copy-start | bytes 110596
  8.0 97.2 %all-gather.7.cloned.1.call-start = ((), (), s32[]{:S(2)}) async-start(), calls=%async_computation.10 | async-start | bytes 4718592 | tf_op jit(solution)/shard_map/all_gather | solution.py:129
  8.8 266.3 %reduce-scatter.17.cloned.1.call-start = ((), (), s32[]{:S(2)}) async-start(), calls=%async_computation.11 | async-start | bytes 4718592 | tf_op jit(solution)/shard_map/reduce_scatter | solution.py:148
  15.4 174.5 %copy-start.125 = (pred[2,1024]{1,0:T(4,128)(4,1)}, pred[2,1024]{1,0:T(4,128)(4,1)S(1)}, u32[]{:S(2)}) copy-start(pred[2,1024]{1,0:T(4,128)(4,1)S(1)} %get-tuple-element.187) | copy-start | bytes 6148
  136.5 59.0 %copy-start.8 = (f32[2,6,1024,64]{2,3,1,0:T(8,128)}, f32[2,6,1024,64]{2,3,1,0:T(8,128)S(1)}, u32[]{:S(2)}) copy-start(f32[2,6,1024,64]{2,3,1,0:T(8,128)S(1)} %get-tuple-element.185) | copy-start | bytes 9437188
  231.5 50.3 %all-gather.11.cloned.1.call-start = ((), (), s32[]{:S(2)}) async-start(), calls=%async_computation.13 | async-start | bytes 2506752 | tf_op jit(solution)/shard_map/all_gather | solution.py:119
  232.0 93.5 %all-gather.9.cloned.1.call-start = ((), (), s32[]{:S(2)}) async-start(), calls=%async_computation.12 | async-start | bytes 4718592 | tf_op jit(solution)/shard_map/all_gather | solution.py:157
  273.2 154.5 %copy-start.153 = (f32[768]{0:T(1024)}, f32[768]{0:T(1024)S(1)}, u32[]{:S(2)}) copy-start(f32[768]{0:T(1024)S(1)} %get-tuple-element.140) | copy-start | bytes 9220
  281.1 89.3 %all-gather.13.cloned.1.call-start = ((), (), s32[]{:S(2)}) async-start(), calls=%async_computation.14 | async-start | bytes 2506752 | tf_op jit(solution)/shard_map/all_gather | solution.py:120
  281.7 139.7 %reduce-scatter.19.cloned.1.call-start = ((), (), s32[]{:S(2)}) async-start(), calls=%async_computation.15 | async-start | bytes 4718592 | tf_op jit(solution)/shard_map/reduce_scatter | solution.py:161
  379.4 98.1 %all-gather.15.cloned.1.call-start = ((), (), s32[]{:S(2)}) async-start(), calls=%async_computation.16 | async-start | bytes 4718592 | tf_op jit(solution)/shard_map/all_gather | solution.py:173
  432.7 111.7 %reduce-scatter.21.cloned.1.call-start = ((), (), s32[]{:S(2)}) async-start(), calls=%async_computation.17 | async-start | bytes 4718592 | tf_op jit(solution)/shard_map/reduce_scatter | solution.py:189
  500.9 99.5 %all-gather.17.cloned.1.call-start = ((), (), s32[]{:S(2)}) async-start(), calls=%async_computation.18 | async-start | bytes 4718592 | tf_op jit(solution)/shard_map/all_gather | solution.py:196
  555.3 430.6 %reduce-scatter.23.cloned.1.call-start = ((), (), s32[]{:S(2)}) async-start(), calls=%async_computation.19 | async-start | bytes 4718592 | tf_op jit(solution)/shard_map/reduce_scatter | solution.py:210
  845.8 143.2 %reduce-scatter.29.cloned.1.call-start = ((), (), s32[]{:S(2)}) async-start(), calls=%async_computation.22 | async-start | bytes 5013504 | tf_op jit(solution)/shard_map/reduce_scatter | solution.py:223
  855.9 193.1 %reduce-scatter.27.cloned.1.call-start = ((), (), s32[]{:S(2)}) async-start(), calls=%async_computation.21 | async-start | bytes 5013504 | tf_op jit(solution)/shard_map/reduce_scatter | solution.py:222
  865.7 244.9 %reduce-scatter.25.cloned.1.call-start = ((), (), s32[]{:S(2)}) async-start(), calls=%async_computation.20 | async-start | bytes 1253376 | tf_op jit(solution)/shard_map/reduce_scatter | solution.py:221
  871.2 300.8 %reduce-scatter.31.cloned.1.call-start = ((), (), s32[]{:S(2)}) async-start(), calls=%async_computation.23 | async-start | bytes 1253376
  879.3 354.0 %reduce-scatter.33.cloned.1.call-start = ((), (), s32[]{:S(2)}) async-start(), calls=%async_computation.24 | async-start | bytes 1253376
  887.5 407.2 %reduce-scatter.35.cloned.1.call-start = ((), (), s32[]{:S(2)}) async-start(), calls=%async_computation.25 | async-start | bytes 1253376
  898.6 83.3 %copy-start.134 = (f32[1024]{0:T(1024)S(1)}, f32[1024]{0:T(1024)}, u32[]{:S(2)}) copy-start(f32[1024]{0:T(1024)} %copy-done.133) | copy-start | bytes 12292
  898.6 83.3 %copy-start.144 = (f32[1024]{0:T(1024)S(1)}, f32[1024]{0:T(1024)}, u32[]{:S(2)}) copy-start(f32[1024]{0:T(1024)} %copy-done.143) | copy-start | bytes 12292
  898.7 83.3 %copy-start.154 = (f32[768]{0:T(1024)S(1)}, f32[768]{0:T(1024)}, u32[]{:S(2)}) copy-start(f32[768]{0:T(1024)} %copy-done.153) | copy-start | bytes 9220
  935.9 50.0 %copy-start.17 = (f32[1024,768]{1,0:T(8,128)S(1)}, f32[1024,768]{1,0:T(8,128)}, u32[]{:S(2)}) copy-start(f32[1024,768]{1,0:T(8,128)} %copy-done.16) | copy-start | bytes 9437188
  (234 other events, 2521.1 us)
Sparse Core Ops, SparseCore 0:
  10.4 47.6 all-gather.6
  231.6 43.4 reduce-scatter.16
  379.5 41.7 reduce-scatter.18
  555.4 44.8 all-gather.16
  846.0 43.4 reduce-scatter.22
  893.7 75.7 reduce-scatter.28
  974.0 75.0 reduce-scatter.26
  1053.2 57.3 reduce-scatter.24
  1114.8 57.1 reduce-scatter.30
  1176.0 57.2 reduce-scatter.32
  1237.5 57.1 reduce-scatter.34
Sparse Core Ops, SparseCore 1:
  234.2 40.7 all-gather.10
  281.2 44.3 all-gather.8
  327.7 42.6 all-gather.12
  432.8 44.7 all-gather.14
  501.0 43.3 reduce-scatter.20
where the time goes:
time: 1310 us; the launch traced here: 1300 us
  waiting for transfers between devices  534 us (41%)
  matrix products  291 us (22%)
  other arithmetic  191 us (15%)
  blocking collectives  171 us (13%)
  local copies, waits for them, and re-layouts  94 us (7%)
  between operations  20.6 us (2%)
    unnamed x19, waiting for transfers between devices  186 us
    dot_general x90, matrix products, exact_einsum_product(): jnp.einsum(formula, left_op, right_op, precision=lax.Precision.HIGHEST)  155 us
    unnamed x2, blocking collectives  81.2 us
    reduce_scatter x1, waiting for transfers between devices, per_device(): lax.psum_scatter(grad_out_full, 'dp', scatter_dimension=1, tiled=True)  61.5 us
    reduce_scatter x1, waiting for transfers between devices, per_device(): lax.psum_scatter(grad_in_full, 'dp', scatter_dimension=0, tiled=True)  60 us
    reduce_sum x2, other arithmetic, nystrom(): conv_taps[:, offset, None, None] * padded[:, offset:offset + length, :]  52.4 us
    all_gather x1, waiting for transfers between devices, per_device(): lax.all_gather(grad_resid_two.astype(jnp.bfloat16), 'tensor', axis=0, til...  44.6 us
    all_gather x1, waiting for transfers between devices, per_device(): hidden_all = lax.all_gather(hidden_low, 'tensor', axis=0, tiled=True)  43.8 us
  transfers between devices with their start and end apart: 16, of which 12 were waited for; matrix products, arithmetic and copies ran while one was open for 12% of the time, Pallas kernels for 0%

commit v1 on v0

v1 whole, which is shorter than its diff:
```python
from functools import partial

import jax
import jax.numpy as jnp
from jax import lax
from jax.experimental import pallas as pl
from jax.experimental.pallas import tpu as pltpu
from jax.sharding import PartitionSpec as P

F32, BF = jnp.float32, jnp.bfloat16
NN, NT, TN = ((1,), (0,)), ((1,), (1,)), ((0,), (0,))
MARKS = 64
HEAD = 64
PACK = 4
WIDE = PACK * HEAD
TAPS = 33
EDGE = TAPS // 2
ROWS = 128
WINDOW = ROWS + 2 * EDGE
STEPS = 6
KEPT = 4


def mm(a, b, dims=NN):
    return lax.dot_general(a, b, (dims, ((), ())), preferred_element_type=F32)


def halves(a):
    high = a.astype(BF)
    return high, (a - high.astype(F32)).astype(BF)


def mm3(a, b, dims=NN):
    (ah, al), (bh, bl) = a, b
    return mm(ah, bh, dims) + (mm(ah, bl, dims) + mm(al, bh, dims))


def mm3f(a, b, dims=NN):
    return mm3(halves(a), halves(b), dims)


def grid_of(shape):
    return (
        lax.broadcasted_iota(jnp.int32, shape, 0),
        lax.broadcasted_iota(jnp.int32, shape, 1),
    )


def block_mask():
    row, col = grid_of((WIDE, WIDE))
    return row // HEAD == col // HEAD


def eye():
    row, col = grid_of((WIDE, WIDE))
    return (row == col).astype(F32)


def spread(packed, mask):
    full = jnp.concatenate([packed] * PACK, axis=0)
    return jnp.where(mask, full, jnp.zeros_like(full))


def gather_up(full):
    return sum(full[i * MARKS : (i + 1) * MARKS] for i in range(PACK))


def segment_reduce(a, fill, op):
    lane = lax.broadcasted_iota(jnp.int32, (a.shape[0], 128), 1) < HEAD
    parts = []
    for tile in range(a.shape[1] // 128):
        piece = a[:, tile * 128 : (tile + 1) * 128]
        low = op(jnp.where(lane, piece, fill), axis=1, keepdims=True)
        high = op(jnp.where(lane, fill, piece), axis=1, keepdims=True)
        parts.append(jnp.where(lane, low, high))
    return jnp.concatenate(parts, axis=1)


def average_matrix():
    row, col = grid_of((ROWS * MARKS // 1024, ROWS))
    return jnp.where(row == col // 16, 1.0 / 16, 0.0).astype(BF)


def average_back():
    row, col = grid_of((ROWS, ROWS * MARKS // 1024))
    return jnp.where(row // 16 == col, 1.0 / 16, 0.0).astype(BF)


def lanes_of(group):
    return slice(group * WIDE, (group + 1) * WIDE)


def toeplitz(taps_ref, group):
    parts = []
    for i in range(PACK):
        head = group * PACK + i
        line = jnp.broadcast_to(taps_ref[head : head + 1, :], (ROWS, 256))
        parts.append(pltpu.roll(line, 0, 1, stride=1, stride_axis=0)[:, :WINDOW])
    return jnp.concatenate(parts, axis=0).astype(BF)


def diagonal_lanes(stacked):
    col = lax.broadcasted_iota(jnp.int32, (ROWS, WIDE), 1) // HEAD
    out = stacked[:ROWS]
    for i in range(1, PACK):
        out = jnp.where(col == i, stacked[i * ROWS : (i + 1) * ROWS], out)
    return out


def attn_fwd_kernel(slot, groups, len_ref, q_ref, k_ref, v_ref, taps_ref,
                    ctx_ref, qh_ref, kh_ref, vp_ref, k1_ref, k3_ref,
                    small_ref, chain_ref,
                    z_ref, k2_ref, s_ref, top_ref, t_ref):
    count = slot // ROWS
    marks = ROWS // 16
    scale = HEAD ** -0.25
    length = len_ref[0]
    avg = average_matrix()
    wide = groups * WIDE
    vp_ref[0:EDGE, :] = jnp.zeros((EDGE, wide), BF)
    vp_ref[slot + EDGE : slot + 2 * EDGE, :] = jnp.zeros((EDGE, wide), BF)

    def load(i, carry):
        rows = pl.ds(pl.multiple_of(i * ROWS, ROWS), ROWS)
        row = lax.broadcasted_iota(jnp.int32, (ROWS, 1), 0) + i * ROWS
        valid = (row < length).astype(F32)
        few = pl.ds(pl.multiple_of(i * marks, marks), marks)
        q = q_ref[rows, :] * (valid * scale)
        high, low = halves(q)
        qh_ref[rows, :] = high
        small_ref[0, few, :] = mm(avg, high) + mm(avg, low)
        k = k_ref[rows, :] * (valid * scale)
        high, low = halves(k)
        kh_ref[rows, :] = high
        small_ref[1, few, :] = mm(avg, high) + mm(avg, low)
        vp_ref[pl.ds(pl.multiple_of(i * ROWS + EDGE, EDGE), ROWS), :] = (
            v_ref[rows, :] * valid
        ).astype(BF)
        return carry

    lax.fori_loop(0, count, load, 0)
    mask = block_mask()
    one = eye()

    for g in range(groups):
        at = lanes_of(g)
        ql, kl = spread(small_ref[0, :, at], mask), spread(small_ref[1, :, at], mask)
        a2 = jnp.where(mask, mm3f(ql, kl, NT), -1e30)
        e2 = jnp.where(mask, jnp.exp(a2 - jnp.max(a2, axis=1, keepdims=True)), 0.0)
        k2 = e2 / jnp.sum(e2, axis=1, keepdims=True)
        top = segment_reduce(jnp.sum(k2, axis=0, keepdims=True), -1e30, jnp.max)
        k2_ref[g] = k2
        small_ref[2, :, at] = gather_up(k2)
        z_ref[g] = jnp.transpose(k2) / top

    def newton(step, carry):
        for g in range(groups):
            at = lanes_of(g)
            z = z_ref[g]
            zs = halves(z)
            p = mm3(halves(k2_ref[g]), zs)
            ps = halves(p)
            t2 = 15.0 * one - mm3(ps, halves(7.0 * one - p))
            t3 = 13.0 * one - mm3(ps, halves(t2))
            chain_ref[step, 0, :, at] = gather_up(z)
            chain_ref[step, 1, :, at] = gather_up(p)
            chain_ref[step, 2, :, at] = gather_up(t2)
            chain_ref[step, 3, :, at] = gather_up(t3)
            z_ref[g] = 0.25 * mm3(zs, halves(t3))
        return carry

    lax.fori_loop(0, STEPS, newton, 0)

    for g in range(groups):
        at = lanes_of(g)
        ql = spread(small_ref[0, :, at], mask).astype(BF)
        top_ref[...] = jnp.full(top_ref.shape, -jnp.inf, F32)

        def scores(i, carry):
            rows = pl.ds(pl.multiple_of(i * ROWS, ROWS), ROWS)
            row = lax.broadcasted_iota(jnp.int32, (ROWS, 1), 0) + i * ROWS
            a3 = jnp.where(row < length, mm(kh_ref[rows, at], ql, NT), -1e9)
            s_ref[rows, :] = a3
            top_ref[0:1, :] = jnp.maximum(top_ref[0:1, :], jnp.max(a3, axis=0, keepdims=True))
            return carry

        lax.fori_loop(0, count, scores, 0)
        peak = top_ref[0:1, :]
        top_ref[0:1, :] = jnp.zeros((1, WIDE), F32)

        def powers(i, carry):
            rows = pl.ds(pl.multiple_of(i * ROWS, ROWS), ROWS)
            e3 = jnp.exp(s_ref[rows, :] - peak)
            s_ref[rows, :] = e3
            top_ref[0:1, :] += jnp.sum(e3, axis=0, keepdims=True)
            return carry

        lax.fori_loop(0, count, powers, 0)
        inverse = 1.0 / top_ref[0:1, :]

        def weigh(i, carry):
            rows = pl.ds(pl.multiple_of(i * ROWS, ROWS), ROWS)
            k3_ref[rows, at] = (s_ref[rows, :] * inverse).astype(BF)
            return carry

        lax.fori_loop(0, count, weigh, 0)
        b = mm(k3_ref[:, at], vp_ref[EDGE : slot + EDGE, at], TN)
        b = jnp.where(mask, b, 0.0)
        z = z_ref[g]
        c = mm3f(z, b)
        small_ref[3, :, at] = gather_up(b)
        small_ref[4, :, at] = gather_up(c)
        small_ref[5, :, at] = gather_up(z)
        t_ref[...] = toeplitz(taps_ref, g)
        cb = c.astype(BF)
        kl = spread(small_ref[1, :, at], mask).astype(BF)
        ones = mask.astype(F32).astype(BF)

        def mix(i, carry):
            rows = pl.ds(pl.multiple_of(i * ROWS, ROWS), ROWS)
            a1 = mm(qh_ref[rows, at], kl, NT)
            e1 = jnp.exp(a1 - segment_reduce(a1, -jnp.inf, jnp.max)).astype(BF)
            k1 = (e1.astype(F32) / mm(e1, ones)).astype(BF)
            k1_ref[rows, at] = k1
            window = vp_ref[pl.ds(pl.multiple_of(i * ROWS, ROWS), WINDOW), at]
            ctx_ref[rows, at] = (
                mm(k1, cb) + diagonal_lanes(mm(t_ref[...], window))
            ).astype(BF)
            return carry

        lax.fori_loop(0, count, mix, 0)


def attn_bwd_kernel(slot, groups, len_ref, g_ref, qh_ref, kh_ref, vp_ref, k1_ref, k3_ref,
                    small_ref, chain_ref, flip_ref,
                    dqkv_ref, conv_ref,
                    gp_ref, da1_ref, da3_ref, dk_ref, dz_ref, k2_ref,
                    dql_ref, dkl_ref, t_ref, acc_ref):
    count = slot // ROWS
    marks = ROWS // 16
    scale = HEAD ** -0.25
    length = len_ref[0]
    wide = groups * WIDE
    mask = block_mask()
    one = eye()
    ones = mask.astype(F32).astype(BF)
    gp_ref[0:EDGE, :] = jnp.zeros((EDGE, wide), BF)
    gp_ref[slot + EDGE : slot + 2 * EDGE, :] = jnp.zeros((EDGE, wide), BF)
    gp_ref[EDGE : slot + EDGE, :] = g_ref[...]
    col = lax.broadcasted_iota(jnp.int32, (ROWS, WIDE), 1) // HEAD
    up, across = grid_of((ROWS, ROWS))
    flip = jnp.where(up + across == ROWS - 1, 1.0, 0.0).astype(BF)

    for g in range(groups):
        at = lanes_of(g)
        c = spread(small_ref[4, :, at], mask)
        cb = c.astype(BF)

        def first(i, carry):
            rows = pl.ds(pl.multiple_of(i * ROWS, ROWS), ROWS)
            k1 = k1_ref[rows, at].astype(F32)
            dk1 = mm(g_ref[rows, at], cb, NT)
            high, low = halves(dk1 * k1)
            da1_ref[rows, at] = (k1 * (dk1 - (mm(high, ones) + mm(low, ones)))).astype(BF)
            return carry

        lax.fori_loop(0, count, first, 0)
        dc = jnp.where(mask, mm(k1_ref[:, at], g_ref[:, at], TN), 0.0)
        dkl_ref[g] = jnp.where(mask, mm(da1_ref[:, at], qh_ref[:, at], TN), 0.0)
        b = spread(small_ref[3, :, at], mask)
        z = spread(small_ref[5, :, at], mask)
        dcs = halves(dc)
        dz_ref[g] = mm3(halves(b), dcs, NT)
        db = mm3(halves(z), dcs, TN)
        dbb = db.astype(BF)
        high, low = halves(db * b)
        many = jnp.ones((8, WIDE), BF)
        total = (mm(many, high, NT) + mm(many, low, NT))[0:1, :]
        t_ref[...] = toeplitz(flip_ref, g)
        acc_ref[...] = jnp.zeros(acc_ref.shape, F32)

        def second(i, carry):
            rows = pl.ds(pl.multiple_of(i * ROWS, ROWS), ROWS)
            row = lax.broadcasted_iota(jnp.int32, (ROWS, 1), 0) + i * ROWS
            valid = (row < length).astype(F32)
            k3 = k3_ref[rows, at]
            vh = vp_ref[pl.ds(pl.multiple_of(i * ROWS + EDGE, EDGE), ROWS), at]
            dk3 = mm(vh, dbb, NT)
            da3_ref[rows, at] = (k3.astype(F32) * (dk3 - total)).astype(BF)
            window = pl.ds(pl.multiple_of(i * ROWS, ROWS), WINDOW)
            dv = mm(k3, dbb) + diagonal_lanes(mm(t_ref[...], gp_ref[window, at]))
            dqkv_ref[rows, 2 * wide + g * WIDE : 2 * wide + (g + 1) * WIDE] = (dv * valid).astype(BF)
            grad = g_ref[rows, at]
            split = jnp.concatenate(
                [jnp.where(col == h, grad, jnp.zeros_like(grad)) for h in range(PACK)], axis=0
            )
            acc_ref[:, :WINDOW] += mm(split, vp_ref[window, at], NT)
            return carry

        lax.fori_loop(0, count, second, 0)
        for h in range(PACK):
            high, low = halves(acc_ref[h * ROWS : (h + 1) * ROWS, :])
            turned = pltpu.roll(mm(flip, high) + mm(flip, low), 0, 1, stride=1, stride_axis=0)
            conv_ref[g * PACK + h : g * PACK + h + 1, :] = jnp.sum(turned, axis=0, keepdims=True)
        dql_ref[g] = jnp.where(mask, mm(da3_ref[:, at], kh_ref[:, at], TN), 0.0)
        dk_ref[g] = jnp.zeros((WIDE, WIDE), F32)
        k2_ref[g] = spread(small_ref[2, :, at], mask)

    def newton(back, carry):
        step = STEPS - 1 - back
        for g in range(groups):
            at = lanes_of(g)
            zs = halves(spread(chain_ref[step, 0, :, at], mask))
            p = spread(chain_ref[step, 1, :, at], mask)
            t2s = halves(spread(chain_ref[step, 2, :, at], mask))
            t3s = halves(spread(chain_ref[step, 3, :, at], mask))
            ps = halves(p)
            t1s = halves(7.0 * one - p)
            dzs = halves(0.25 * dz_ref[g])
            dt3 = halves(mm3(dzs, zs))
            dp = -mm3(t2s, dt3)
            dt2f = -mm3(dt3, ps)
            dt2 = halves(dt2f)
            dp = dp - mm3(t1s, dt2) + mm3(dt2, ps)
            dps = halves(dp)
            dk_ref[g] += mm3(zs, dps)
            dz_ref[g] = mm3(t3s, dzs) + mm3(dps, halves(k2_ref[g]))
        return carry

    lax.fori_loop(0, STEPS, newton, 0)

    for g in range(groups):
        at = lanes_of(g)
        k2 = k2_ref[g]
        sums = jnp.sum(k2, axis=0, keepdims=True)
        top = segment_reduce(sums, -1e30, jnp.max)
        hit = (sums == top).astype(F32)
        ties = segment_reduce(hit, 0.0, jnp.sum)
        dz0 = dz_ref[g]
        dtop = -segment_reduce(jnp.sum(dz0 * k2, axis=0, keepdims=True), 0.0, jnp.sum) / (top * top)
        dk2 = jnp.transpose(dk_ref[g]) + dz0 / top + hit * (dtop / ties)
        dk2 = jnp.where(mask, dk2, 0.0)
        da2 = k2 * (dk2 - jnp.sum(dk2 * k2, axis=1, keepdims=True))
        da2s = halves(da2)
        ql, kl = spread(small_ref[0, :, at], mask), spread(small_ref[1, :, at], mask)
        qls, kls = halves(ql), halves(kl)
        dql = gather_up(dql_ref[g] + mm3(da2s, kls))
        dkl = gather_up(dkl_ref[g] + mm3(da2s, qls, TN))
        dql_ref[g, 0:MARKS, :] = dql
        dkl_ref[g, 0:MARKS, :] = dkl
        qlb, klb = qls[0], kls[0]
        back = average_back()

        def third(i, carry):
            rows = pl.ds(pl.multiple_of(i * ROWS, ROWS), ROWS)
            few = pl.ds(pl.multiple_of(i * marks, marks), marks)
            row = lax.broadcasted_iota(jnp.int32, (ROWS, 1), 0) + i * ROWS
            valid = jnp.where(row < length, scale, 0.0)
            dq = mm(da1_ref[rows, at], klb) + mm(back, dql_ref[g, few, :].astype(BF))
            dk = mm(da3_ref[rows, at], qlb) + mm(back, dkl_ref[g, few, :].astype(BF))
            dqkv_ref[rows, g * WIDE : (g + 1) * WIDE] = (dq * valid).astype(BF)
            dqkv_ref[rows, wide + g * WIDE : wide + (g + 1) * WIDE] = (dk * valid).astype(BF)
            return carry

        lax.fori_loop(0, count, third, 0)


VM = pl.BlockSpec(memory_space=pltpu.VMEM)
SM = pl.BlockSpec(memory_space=pltpu.SMEM)
LIMIT = 60 * 1024 * 1024


def attn_fwd(length, q, k, v, taps):
    slot, wide = q.shape
    groups = wide // WIDE
    shape = jax.ShapeDtypeStruct
    return pl.pallas_call(
        partial(attn_fwd_kernel, slot, groups),
        out_shape=(
            shape((slot, wide), BF),
            shape((slot, wide), BF),
            shape((slot, wide), BF),
            shape((slot + 2 * EDGE, wide), BF),
            shape((slot, wide), BF),
            shape((slot, wide), BF),
            shape((6, MARKS, wide), F32),
            shape((STEPS, KEPT, MARKS, wide), F32),
        ),
        in_specs=[SM, VM, VM, VM, VM],
        out_specs=[VM] * 8,
        scratch_shapes=[
            pltpu.VMEM((groups, WIDE, WIDE), F32),
            pltpu.VMEM((groups, WIDE, WIDE), F32),
            pltpu.VMEM((slot, WIDE), F32),
            pltpu.VMEM((8, WIDE), F32),
            pltpu.VMEM((PACK * ROWS, WINDOW), BF),
        ],
        compiler_params=pltpu.CompilerParams(vmem_limit_bytes=LIMIT),
        name="attn_fwd",
    )(length, q, k, v, taps)


def attn_bwd(length, g, qh, kh, vp, k1, k3, small, chain, flip):
    slot, wide = g.shape
    groups = wide // WIDE
    shape = jax.ShapeDtypeStruct
    return pl.pallas_call(
        partial(attn_bwd_kernel, slot, groups),
        out_shape=(shape((slot, 3 * wide), BF), shape((16, 256), F32)),
        in_specs=[SM] + [VM] * 9,
        out_specs=[VM] * 2,
        scratch_shapes=[
            pltpu.VMEM((slot + 2 * EDGE, wide), BF),
            pltpu.VMEM((slot, wide), BF),
            pltpu.VMEM((slot, wide), BF),
            pltpu.VMEM((groups, WIDE, WIDE), F32),
            pltpu.VMEM((groups, WIDE, WIDE), F32),
            pltpu.VMEM((groups, WIDE, WIDE), F32),
            pltpu.VMEM((groups, WIDE, WIDE), F32),
            pltpu.VMEM((groups, WIDE, WIDE), F32),
            pltpu.VMEM((PACK * ROWS, WINDOW), BF),
            pltpu.VMEM((PACK * ROWS, 256), F32),
        ],
        compiler_params=pltpu.CompilerParams(vmem_limit_bytes=LIMIT),
        name="attn_bwd",
    )(length, g, qh, kh, vp, k1, k3, small, chain, flip)


D = 768
BOTH = ("tensor", "dp")


def rows_sum(left_op, right_op):
    return lax.dot_general(left_op, right_op, (TN, ((), ())), preferred_element_type=F32)


def cols_sum(left_op, right_op):
    return lax.dot_general(left_op, right_op, (NT, ((), ())), preferred_element_type=F32)


def dense(left_op, right_op):
    return jnp.dot(left_op, right_op, preferred_element_type=F32)


def norm_parts(values):
    centre = values - jnp.mean(values, axis=-1, keepdims=True)
    spread_of = jnp.mean(centre * centre, axis=-1, keepdims=True)
    inverse = lax.rsqrt(spread_of + 1e-05)
    return centre * inverse, inverse


def norm_back(grad, gain, normal, inverse):
    scaled = grad * gain
    lean = jnp.mean(scaled, axis=-1, keepdims=True)
    along = jnp.mean(scaled * normal, axis=-1, keepdims=True)
    return (
        inverse * (scaled - lean - normal * along),
        jnp.sum(grad * normal, axis=0),
        jnp.sum(grad, axis=0),
    )


def gather_weights(pieces):
    joined = lax.all_gather(jnp.concatenate(pieces, axis=1), BOTH, axis=0, tiled=True)
    halves_of = lax.axis_size("tensor")
    joined = joined.reshape(halves_of, D, -1)
    whole, start = [], 0
    for piece in pieces:
        width = piece.shape[1]
        part = joined[:, :, start : start + width]
        whole.append(part.transpose(1, 0, 2).reshape(D, halves_of * width))
        start += width
    return whole


def scatter_grads(fulls):
    halves_of = lax.axis_size("tensor")
    stacked = jnp.concatenate(
        [
            jnp.concatenate(
                [
                    full[:, t * full.shape[1] // halves_of : (t + 1) * full.shape[1] // halves_of]
                    for t in range(halves_of)
                ],
                axis=0,
            )
            for full in fulls
        ],
        axis=1,
    )
    mine = lax.psum_scatter(stacked, BOTH, scatter_dimension=0, tiled=True)
    out, start = [], 0
    for full in fulls:
        width = full.shape[1] // halves_of
        out.append(mine[:, start : start + width].astype(F32))
        start += width
    return out


def per_device(x_in, lengths, cotangent, w_query, w_key, w_value, w_out, w_in, w_down,
               conv_weight, ln1_gain, ln1_bias, ln2_gain, ln2_bias):
    tensor_index = lax.axis_index("tensor")
    slot = x_in.shape[0]
    halves_of = lax.axis_size("tensor")
    length = lax.dynamic_slice_in_dim(lengths, tensor_index, 1)
    valid = (jnp.arange(slot, dtype=jnp.int32) < length[0]).astype(F32)[:, None]

    query_w, key_w, value_w = gather_weights((w_query, w_key, w_value))
    out_w, in_w, down_w = gather_weights((w_out.T, w_in, w_down.T))
    gains = lax.all_gather(
        jnp.stack([ln1_gain, ln1_bias, ln2_gain, ln2_bias]), ("dp", "tensor"), axis=1, tiled=True
    )
    gain_one, bias_one, gain_two, bias_two = gains[0], gains[1], gains[2], gains[3]
    taps = lax.all_gather(conv_weight, "tensor", axis=0, tiled=True)
    heads, count = taps.shape
    room = ((0, 16 - heads), (0, 256 - count))

    tokens = x_in.astype(F32)
    queries, keys_all, values_all = dense(x_in, query_w), dense(x_in, key_w), dense(x_in, value_w)
    ctx, qh, kh, vp, k1, k3, small, chain = attn_fwd(
        length, queries, keys_all, values_all, jnp.pad(taps, room)
    )
    attn_branch = cols_sum(ctx, out_w)
    normal_one, inverse_one = norm_parts(tokens + attn_branch)
    hidden = (normal_one * gain_one + bias_one).astype(BF)
    pre = dense(hidden, in_w)
    below = 0.5 * (1.0 + lax.erf(pre * 0.5**0.5))
    act = (pre * below).astype(BF)
    slope = (below + pre * jnp.exp(-0.5 * pre * pre) * (2.0 * jnp.pi) ** -0.5).astype(BF)
    ffn_branch = cols_sum(act, down_w)
    normal_two, inverse_two = norm_parts(hidden.astype(F32) + ffn_branch)
    output = (normal_two * gain_two + bias_two).astype(BF)
    grad_result = cotangent.astype(F32) * valid
    d_res2, grad_gain_two, grad_bias_two = norm_back(grad_result, gain_two, normal_two, inverse_two)
    d_ffn = d_res2.astype(BF)
    grad_down = rows_sum(d_ffn, act)
    d_pre = (dense(d_ffn, down_w) * slope.astype(F32)).astype(BF)
    grad_in = rows_sum(hidden, d_pre)
    d_hidden = cols_sum(d_pre, in_w) + d_res2
    d_res1, grad_gain_one, grad_bias_one = norm_back(d_hidden, gain_one, normal_one, inverse_one)
    d_attn = d_res1.astype(BF)
    grad_out = rows_sum(d_attn, ctx)
    d_ctx = dense(d_attn, out_w).astype(BF)
    early = scatter_grads([grad_out.astype(BF), grad_in.astype(BF), grad_down.astype(BF)])
    d_qkv, conv_rows = attn_bwd(
        length, d_ctx, qh, kh, vp, k1, k3, small, chain, jnp.pad(taps[:, ::-1], room)
    )
    qkv_w = jnp.concatenate([query_w, key_w, value_w], axis=1)
    input_grad = (d_res1 + cols_sum(d_qkv, qkv_w)).astype(BF)
    grad_qkv = rows_sum(x_in, d_qkv).astype(BF)
    late = scatter_grads([grad_qkv[:, :D], grad_qkv[:, D : 2 * D], grad_qkv[:, 2 * D :]])

    def total(branch):
        return jnp.sum(valid * branch * branch)

    summed = lax.psum(
        jnp.concatenate(
            [
                grad_gain_one, grad_bias_one, grad_gain_two, grad_bias_two,
                conv_rows[:heads, ROWS - 1 : ROWS - 1 + count].reshape(-1),
                jnp.stack([total(tokens), total(attn_branch), total(ffn_branch), jnp.sum(valid)]),
            ]
        ),
        ("dp", "tensor"),
    )
    share = D // lax.axis_size(("dp", "tensor"))
    start_at = lax.axis_index(("dp", "tensor")) * share
    vectors = lax.dynamic_slice_in_dim(summed[: 4 * D].reshape(4, D), start_at, share, 1)
    conv_all = summed[4 * D : 4 * D + heads * count].reshape(heads, count)
    own_heads = heads // halves_of
    conv_grad = lax.dynamic_slice_in_dim(conv_all, tensor_index * own_heads, own_heads, 0)
    sums = summed[4 * D + heads * count :]
    stats = jnp.sqrt(sums[:3] / (sums[3] * D))
    return (
        output, input_grad, late[0], late[1], late[2], early[0].T, early[1], early[2].T,
        conv_grad, vectors[0], vectors[1], vectors[2], vectors[3], stats,
    )


def solution(mesh):
    rows, both = P(("dp", "tensor"), None), P(("dp", "tensor"))
    split, crossed = P("dp", "tensor"), P("tensor", "dp")
    return jax.shard_map(
        per_device,
        mesh=mesh,
        in_specs=(rows, P("dp"), rows, split, split, split, crossed, split, crossed,
                  P("tensor", None), both, both, both, both),
        out_specs=(rows, rows, split, split, split, crossed, split, crossed,
                   P("tensor", None), both, both, both, both, P()),
        check_vma=False,
    )
```

time: 1310 us -> 616 us (0.47)
  waiting for transfers between devices: 534 us -> 120 us
  matrix products: 291 us -> 92.6 us
  Pallas kernels: 0 us -> 112 us
  other arithmetic: 191 us -> 94 us
  blocking collectives: 171 us -> 113 us
  local copies, waits for them, and re-layouts: 94 us -> 58.4 us
    dot_general x108 -> x14, matrix products: 291 us -> 92.6 us  [the longest x6 37.6 us: dense(): return jnp.dot(left_op, right_op, preferred_element_type=F32)]
    unnamed x19 -> x4, waiting for transfers between devices: 186 us -> 0.07 us
    all_gather x6 -> x2, waiting for transfers between devices: 140 us -> 0.01 us  [gather_weights(): lax.all_gather(jnp.concatenate(pieces, axis=1), BOTH, axis=0, tiled=True)]
    pallas_call x0 -> x2, Pallas kernels: none -> 112 us  [the longest x1 58.6 us: attn_bwd(): pl.pallas_call(partial(attn_bwd_kernel, slot, groups), out_shape=(shape((...]
    reduce_scatter x7 -> x2, waiting for transfers between devices: 207 us -> 120 us  [scatter_grads(): mine = lax.psum_scatter(stacked, BOTH, scatter_dimension=0, tiled=True)]
    unnamed x2 -> x0, blocking collectives: 81.2 us -> none
    concatenate x0 -> x4, other arithmetic: none -> 77.1 us  [the longest x2 73.8 us: scatter_grads(): jnp.concatenate([jnp.concatenate([full[:, t * full.shape[1] // halves_of:...]
    reduce_sum x15 -> x4, other arithmetic: 82.4 us -> 8.06 us  [the longest x1 5.88 us: total(): return jnp.sum(valid * branch * branch)]
  transfers between devices with their start and end apart: 16 -> 4, of which waited for: 12 -> 1; matrix products, arithmetic and copies ran while one was open for 12% -> 18% of each run, Pallas kernels for 0% -> 9%
where the time goes in v1:
time: 616 us; the launch traced here: 606 us
  waiting for transfers between devices  120 us (19%)
  blocking collectives  113 us (18%)
  Pallas kernels  112 us (18%)
  other arithmetic  94 us (15%)
  matrix products  92.6 us (15%)
  local copies, waits for them, and re-layouts  58.4 us (9%)
  between operations  15.2 us (2%)
    reduce_scatter x2, waiting for transfers between devices, scatter_grads(): mine = lax.psum_scatter(stacked, BOTH, scatter_dimension=0, tiled=True)  120 us
    concatenate x2, other arithmetic, scatter_grads(): jnp.concatenate([jnp.concatenate([full[:, t * full.shape[1] // halves_of:...  73.8 us
    all_gather x1, blocking collectives, per_device(): lax.all_gather(jnp.stack([ln1_gain, ln1_bias, ln2_gain, ln2_bias]), ('dp'...  68.5 us
    pallas_call x1, Pallas kernels, attn_bwd(): pl.pallas_call(partial(attn_bwd_kernel, slot, groups), out_shape=(shape((...  58.6 us
    pallas_call x1, Pallas kernels, attn_fwd(): pl.pallas_call(partial(attn_fwd_kernel, slot, groups), out_shape=(shape((...  53.8 us
    psum x1, blocking collectives, per_device(): lax.psum(jnp.concatenate([grad_gain_one, grad_bias_one, grad_gain_two, gr...  39.1 us
    dot_general x6, matrix products, dense(): return jnp.dot(left_op, right_op, preferred_element_type=F32)  37.6 us
    dot_general x4, matrix products, cols_sum(): lax.dot_general(left_op, right_op, (NT, ((), ())), preferred_element_type...  33.3 us
  transfers between devices with their start and end apart: 4, of which 1 were waited for; matrix products, arithmetic and copies ran while one was open for 18% of the time, Pallas kernels for 9%

profile of v1, /device:TPU:0, one launch (start us, length us, event | category | flops | bytes accessed | tf_op | source)
XLA Modules:
  0.0 606.0 jit_solution(9440249724880672120)
XLA Ops:
  10.7 5.5 all-gather
  19.5 68.5 %all-gather.1 = f32[32,24,4]{1,2,0:T(4,128)S(1)} all-gather(f32[1,24,4]{1,2,0:T(4,128)S(1)} %maximum_bitcast_fusion), channel_id=1, replica_groups=mesh['dp'=16,'tensor'=2] {'dp','tensor'}, dimensions={0}, use_global_device_ids=true | all-gather | bytes 12672 | tf_op jit(solution)/shard_map/all_gather | solution.py:510
  98.3 4.9 convolution_bitcast_fusion.v_ref
  103.2 3.0 convolution_bitcast_fusion.1.k_ref
  106.2 3.2 convolution_bitcast_fusion.2.q_ref
  109.4 53.8 %attn_fwd.1 = (bf16[1024,768]{1,0:T(8,128)(2,1)}, bf16[1024,768]{1,0:T(8,128)(2,1)}, bf16[1024,768]{1,0:T(8,128)(2,1)}, bf16[1056,768]{1,0:T(8,128)(2,1)}, bf16[...) custom-call(s32[1]{0:T(128)} %dynamic_slice.9.len_ref, ...), custom_call_target="tpu_custom_call" | custom-call | tf_op jit(solution)/shard_map/attn_fwd/pallas_call | solution.py:377
  164.6 8.0 %slice_bitcast_fusion = (bf16[768,2,1536]{2,0,1:T(8,128)(2,1)}, bf16[768,2,1536]{2,0,1:T(8,128)(2,1)}) fusion(bf16[2,768,3456]{2,1,0:T(8,128)(2,1)} %bitcast.82), kind=kLoop, calls=%fused_computation.16 | loop fusion | bytes 18874368 | tf_op jit(solution)/shard_map/transpose | solution.py:471
  174.2 5.4 fusion.29
  180.0 6.6 %copy.72 = bf16[768,2,1536]{0,2,1:T(8,128)(2,1)} copy(bf16[768,2,1536]{2,0,1:T(8,128)(2,1)} %get-tuple-element.114) | data formatting | bytes 9437184 | tf_op jit(solution)/shard_map/transpose | solution.py:471
  186.6 6.7 %copy.73 = bf16[768,2,1536]{0,2,1:T(8,128)(2,1)} copy(bf16[768,2,1536]{2,0,1:T(8,128)(2,1)} %get-tuple-element.113) | data formatting | bytes 9437184 | tf_op jit(solution)/shard_map/transpose | solution.py:471
  193.3 12.1 %multiply_convert_fusion.1 = (bf16[1024,3072]{1,0:T(8,128)(2,1)}, f32[1024,3072]{1,0:T(8,128)}) fusion(bf16[768,3072]{0,1:T(8,128)(2,1)} %bitcast.85, f32[1024,768]{0,1:T(8,128)S(1)} %get-tuple-element.112, f32[768]{0:T(1024)S(1)} %copy-done.21, f32[768]{0:T(1024)S(1)} %get-tuple-element.101, f32[1024]{0:T(1024)S(1)} %add_rsqrt_fusion.1, ...), kind=kOutput, calls=%fused_computation.7 | convolution fusion | flops 4851499008 | bytes 26753024 | tf_op jit(solution)/shard_map/dot_general | solution.py:442
  205.4 9.0 %fusion.28 = (f32[1024]{0:T(1024)S(1)}, f32[1024,768]{0,1:T(8,128)S(1)}, f32[1024,768]{0,1:T(8,128)}) fusion(bf16[1024,3072]{1,0:T(8,128)(2,1)} %get-tuple-element.141, bf16[768,3072]{0,1:T(8,128)(2,1)S(1)} %bitcast.89, f32[768]{0:T(1024)S(1)} %copy-done.21, f32[768]{0:T(1024)S(1)} %get-tuple-element.101, f32[1024]{0:T(1024)S(1)} %add_rsqrt_fusion.1, ...), kind=kOutput, calls=%fused_computation.96 | convolution fusion | flops 4838128640 | bytes 20465664 | tf_op jit(solution)/shard_map/dot_general | solution.py:438
  217.4 5.9 fusion.14
  223.3 11.7 %multiply_convert_fusion = bf16[1024,3072]{1,0:T(8,128)(2,1)} fusion(bf16[768,3072]{0,1:T(8,128)(2,1)S(1)} %bitcast.92, f32[1024,3072]{1,0:T(8,128)} %get-tuple-element.142, bf16[1024,768]{0,1:T(8,128)(2,1)S(1)} %copy-done.7, f32[1024,768]{0,1:T(8,128)S(1)} %get-tuple-element.110, f32[1024]{0:T(1024)S(1)} %get-tuple-element.145, ...), kind=kOutput, calls=%fused_computation.6 | convolution fusion | flops 4877451264 | bytes 28335104 | tf_op jit(solution)/shard_map/dot_general | solution.py:442
  235.1 10.2 %multiply_reduce_fusion.1 = (f32[768]{0:T(1024)S(1)}, f32[1024]{0:T(1024)S(1)}, f32[1024]{0:T(1024)S(1)}, f32[768]{0:T(1024)S(1)}, f32[1024,768]{0,1:T(8,128)}) fusion(f32[1024,768]{0,1:T(8,128)S(1)} %get-tuple-element.112, f32[1024]{0:T(1024)S(1)} %add_rsqrt_fusion.1, f32[1024]{0:T(1024)S(1)} %broadcast_multiply_fusion.5, f32[768]{0:T(1024)S(1)} %get-tuple-element.101, ...), kind=kOutput, calls=%fused_computation.31 | convolution fusion | flops 4846776320 | bytes 22069248 | tf_op jit(solution)/shard_map/dot_general | solution.py:438
  253.2 5.5 convolution_convert_fusion.1
  262.3 58.6 %attn_bwd.1 = (bf16[1024,2304]{1,0:T(8,128)(2,1)}, f32[16,256]{1,0:T(8,128)}) custom-call(s32[1]{0:T(128)} %dynamic_slice.9.len_ref, bf16[1024,768]{1,0:T(8,128)(2,1)} %convolution_convert_fusion.3.g_ref, bf16[1024,768]{1,0:T(8,128)(2,1)} %get-tuple-element.25.qh_ref, bf16[1024,768]{1,0:T(8,128)(2,1)} %get-tuple-element.26.kh_ref, ...), custom_call_target="tpu_custom_call" | custom-call | tf_op jit(solution)/shard_map/attn_bwd/pallas_call | solution.py:407
  320.9 6.5 %fusion.5 = bf16[768,2304]{1,0:T(8,128)(2,1)S(1)} fusion(bf16[1024,2304]{1,0:T(8,128)(2,1)} %get-tuple-element.32, bf16[1024,768]{1,0:T(8,128)(2,1)S(1)} %copy-done.17), kind=kOutput, calls=%fused_computation.18 | convolution fusion | flops 3625648128 | bytes 9830400 | tf_op jit(solution)/shard_map/dot_general | solution.py:434
  327.8 19.1 %maximum_maximum_fusion.1 = bf16[1536,1152]{1,0:T(8,128)(2,1)} fusion(bf16[768,384]{1,0:T(8,128)(2,1)S(1)} %get-tuple-element.120, bf16[768,384]{1,0:T(8,128)(2,1)S(1)} %get-tuple-element.121, bf16[768,384]{1,0:T(8,128)(2,1)S(1)} %get-tuple-element.122, bf16[768,384]{1,0:T(8,128)(2,1)S(1)} %get-tuple-element.123, ...), kind=kLoop, calls=%fused_computation.26 | loop fusion | flops 21233664 | bytes 7077888 | tf_op jit(solution)/shard_map/concatenate | solution.py:478
  348.7 8.4 %convolution_convert_fusion = bf16[768,3072]{1,0:T(8,128)(2,1)S(1)} fusion(bf16[1024,3072]{1,0:T(8,128)(2,1)} %get-tuple-element.141, bf16[1024,768]{0,1:T(8,128)(2,1)} %copy.74, f32[1024,768]{0,1:T(8,128)S(1)} %copy-done.2, f32[1024]{0:T(1024)S(1)} %get-tuple-element.145, f32[1024]{0:T(1024)S(1)} %get-tuple-element.146, f32[1024]{0:T(1024)S(1)} %fusion.24, ...), kind=kOutput, calls=%fused_computation.10 | convolution fusion | flops 4842061824 | bytes 15752192 | tf_op jit(solution)/shard_map/dot_general | solution.py:434
  359.9 54.7 %maximum_maximum_fusion = bf16[1536,3456]{1,0:T(8,128)(2,1)} fusion(bf16[768,1536]{1,0:T(8,128)(2,1)S(1)} %get-tuple-element.118, bf16[768,1536]{1,0:T(8,128)(2,1)S(1)} %get-tuple-element.117, bf16[768,1536]{1,0:T(8,128)(2,1)S(1)} %copy-done.5, bf16[768,1536]{1,0:T(8,128)(2,1)S(1)} %copy-done.4, bf16[768,384]{1,0:T(8,128)(2,1)S(1)} %copy-done.13, ...), kind=kLoop, calls=%fused_computation.9 | loop fusion | flops 63700992 | bytes 21233664 | tf_op jit(solution)/shard_map/concatenate | solution.py:478
  418.9 39.1 %psum.7 = f32[3472]{0:T(1024)S(1)} all-reduce(f32[3472]{0:T(1024)S(1)} %concatenate.47), channel_id=1, replica_groups=mesh['dp'=16,'tensor'=2] {'dp','tensor'}, use_global_device_ids=true, to_apply=%region_18.19 | all-reduce | flops 3472 | bytes 27776 | tf_op jit(solution)/shard_map/psum | solution.py:556
  458.6 8.8 %add_convert_fusion = bf16[1024,768]{0,1:T(8,128)(2,1)} fusion(f32[1024,768]{0,1:T(8,128)S(1)} %copy-done.11, bf16[1024,2304]{1,0:T(8,128)(2,1)} %get-tuple-element.32, bf16[768,768]{0,1:T(8,128)(2,1)} %bitcast.94, bf16[768,768]{0,1:T(8,128)(2,1)} %bitcast.96, bf16[768,768]{0,1:T(8,128)(2,1)} %bitcast.99), kind=kOutput, calls=%fused_computation.32 | convolution fusion | flops 3636068352 | bytes 12976128 | tf_op jit(solution)/shard_map/dot_general | solution.py:438
  475.6 120.2 %reduce-scatter.5.cloned.1.call-done = bf16[48,3456]{1,0:T(8,128)(2,1)} async-done(((bf16[1536,3456]{1,0:T(8,128)(2,1)}), bf16[48,3456]{1,0:T(8,128)(2,1)}) %reduce-scatter.5.cloned.1.call-update) | async-done | bytes 331792 | tf_op jit(solution)/shard_map/reduce_scatter | solution.py:491
  (136 shorter events, 55.6 us)
Async XLA Ops:
  7.2 12.3 %copy-start.26 = (f32[24]{0:T(128)S(1)}, f32[24]{0:T(128)}, u32[]{:S(2)}) copy-start(f32[24]{0:T(128)} %param.24) | copy-start | bytes 292
  7.2 12.3 %copy-start.25 = (f32[24]{0:T(128)S(1)}, f32[24]{0:T(128)}, u32[]{:S(2)}) copy-start(f32[24]{0:T(128)} %param.25) | copy-start | bytes 292
  7.2 12.3 %copy-start.24 = (f32[24]{0:T(128)S(1)}, f32[24]{0:T(128)}, u32[]{:S(2)}) copy-start(f32[24]{0:T(128)} %param.26) | copy-start | bytes 292
  7.2 12.3 %copy-start.23 = (f32[24]{0:T(128)S(1)}, f32[24]{0:T(128)}, u32[]{:S(2)}) copy-start(f32[24]{0:T(128)} %param.27) | copy-start | bytes 292
  7.2 80.9 %copy-start.15 = (bf16[1024,768]{1,0:T(8,128)(2,1)S(1)}, bf16[1024,768]{1,0:T(8,128)(2,1)}, u32[]{:S(2)}) copy-start(bf16[1024,768]{1,0:T(8,128)(2,1)} %param.16) | copy-start | bytes 4718596
  7.2 85.0 %all-gather.5.cloned.1.call-start = ((), (), s32[]{:S(2)}) async-start(), calls=%async_computation.2 | async-start | bytes 3649536 | tf_op jit(solution)/shard_map/all_gather | solution.py:464
  8.9 154.4 %all-gather.7.cloned.1.call-start = ((), (), s32[]{:S(2)}) async-start(), calls=%async_computation.3 | async-start | bytes 10948608 | tf_op jit(solution)/shard_map/all_gather | solution.py:464
  10.7 463.5 %reduce-scatter.3.cloned.1.call-start = ((), (), s32[]{:S(2)}) async-start(), calls=%async_computation.4 | async-start | bytes 3649536 | tf_op jit(solution)/shard_map/reduce_scatter | solution.py:491
  16.9 73.5 %copy-start.27 = (s32[2]{0:T(128)S(1)}, s32[2]{0:T(128)}, u32[]{:S(2)}) copy-start(s32[2]{0:T(128)} %param.15) | copy-start | bytes 28
  98.2 8.0 %copy-start.20 = (bf16[768,2,384]{0,2,1:T(8,128)(2,1)}, bf16[768,2,384]{0,2,1:T(8,128)(2,1)S(1)}, u32[]{:S(2)}) copy-start(bf16[768,2,384]{0,2,1:T(8,128)(2,1)S(1)} %copy.64) | copy-start | bytes 3538948
  98.3 4.9 copy-start.16
  98.3 4.9 copy-start.19
  186.6 6.7 %copy-start.21 = (f32[768]{0:T(1024)S(1)}, f32[768]{0:T(1024)}, u32[]{:S(2)}) copy-start(f32[768]{0:T(1024)} %get-tuple-element.100) | copy-start | bytes 9220
  193.3 12.1 %copy-start.9 = (bf16[768,2,1536]{0,2,1:T(8,128)(2,1)S(1)}, bf16[768,2,1536]{0,2,1:T(8,128)(2,1)}, u32[]{:S(2)}) copy-start(bf16[768,2,1536]{0,2,1:T(8,128)(2,1)} %copy.73) | copy-start | bytes 14155780
  205.4 9.4 %copy-start.3 = (f32[1024,768]{0,1:T(8,128)S(1)}, f32[1024,768]{0,1:T(8,128)}, u32[]{:S(2)}) copy-start(f32[1024,768]{0,1:T(8,128)} %get-tuple-element.140) | copy-start | bytes 9437188
  214.4 20.6 %copy-start.1 = (f32[1024,768]{0,1:T(8,128)}, f32[1024,768]{0,1:T(8,128)S(1)}, u32[]{:S(2)}) copy-start(f32[1024,768]{0,1:T(8,128)S(1)} %get-tuple-element.110) | copy-start | bytes 9437188
  214.4 8.9 %slice-start.2 = ((s8[4718592]{0:T(1024)(128)(4,1)}), s8[4194304]{0:T(1024)(128)(4,1)S(1)}, s32[]{:S(2)}) async-start(s8[4718592]{0:T(1024)(128)(4,1)} %bitcast.90), calls=%async_computation.8 | async-start | bytes 8388608
  217.4 5.9 slice-start.3
  217.4 17.6 %slice-start = ((s8[4718592]{0:T(1024)(128)(4,1)}), s8[4194304]{0:T(1024)(128)(4,1)S(1)}, s32[]{:S(2)}) async-start(s8[4718592]{0:T(1024)(128)(4,1)} %bitcast.86), calls=%async_computation.6 | async-start | bytes 8388608
  223.3 11.7 %slice-start.1 = ((s8[4718592]{0:T(1024)(128)(4,1)}), s8[524288]{0:T(1024)(128)(4,1)S(1)}, s32[]{:S(2)}) async-start(s8[4718592]{0:T(1024)(128)(4,1)} %bitcast.86), calls=%async_computation.7 | async-start | bytes 1048576
  248.1 4.4 slice-start.4
  262.3 58.6 %copy-start.17 = (bf16[1024,768]{1,0:T(8,128)(2,1)S(1)}, bf16[1024,768]{1,0:T(8,128)(2,1)}, u32[]{:S(2)}) copy-start(bf16[1024,768]{1,0:T(8,128)(2,1)} %param.14) | copy-start | bytes 4718596
  346.9 248.9 %reduce-scatter.5.cloned.1.call-start = ((), (), s32[]{:S(2)}) async-start(), calls=%async_computation.5 | async-start | bytes 10948608 | tf_op jit(solution)/shard_map/reduce_scatter | solution.py:491
  414.6 44.0 %copy-start.11 = (f32[1024,768]{0,1:T(8,128)S(1)}, f32[1024,768]{0,1:T(8,128)}, u32[]{:S(2)}) copy-start(f32[1024,768]{0,1:T(8,128)} %copy-done.10) | copy-start | bytes 9437188
  (14 other events, 33.8 us)
Sparse Core Ops, SparseCore 0:
  11.5 62.8 all-gather.4
  77.3 85.3 all-gather.6
  347.0 101.4 reduce-scatter.2
  454.4 141.3 reduce-scatter.4

commit v2 on v1

--- a/solution.py
+++ b/solution.py
@@ -7,6 +7,7 @@
 from jax.experimental.pallas import tpu as pltpu
 from jax.sharding import PartitionSpec as P
 
+ANY = pl.BlockSpec(memory_space=pl.ANY)
 F32, BF = jnp.float32, jnp.bfloat16
 NN, NT, TN = ((1,), (0,)), ((1,), (1,)), ((0,), (0,))
 MARKS = 64
@@ -90,6 +91,22 @@
     return slice(group * WIDE, (group + 1) * WIDE)
 
 
+def picked(ref, rows, which, wide, parts):
+    share = wide // parts
+    return jnp.concatenate(
+        [ref[rows, (3 * p + which) * share : (3 * p + which + 1) * share] for p in range(parts)],
+        axis=1,
+    )
+
+
+def put(ref, rows, which, wide, parts, start, value):
+    share = wide // parts
+    for tile in range(0, value.shape[1], 128):
+        lane = start + tile
+        at = (3 * (lane // share) + which) * share + lane % share
+        ref[rows, at : at + 128] = value[:, tile : tile + 128]
+
+
 def toeplitz(taps_ref, group):
     parts = []
     for i in range(PACK):
@@ -107,10 +124,24 @@
     return out
 
 
-def attn_fwd_kernel(slot, groups, len_ref, q_ref, k_ref, v_ref, taps_ref,
-                    ctx_ref, qh_ref, kh_ref, vp_ref, k1_ref, k3_ref,
-                    small_ref, chain_ref,
-                    z_ref, k2_ref, s_ref, top_ref, t_ref):
+def attn_fwd_kernel(slot, groups, parts, cuts, *refs):
+    n = 0 if cuts is None else max(c[0] for c in cuts) + 1
+    len_ref, qkv_ref, taps_ref = refs[:3]
+    shards, wholes = refs[3 : 3 + n], refs[3 + n : 3 + 2 * n]
+    ctx_ref, qh_ref, kh_ref, vp_ref, k1_ref, k3_ref, small_ref, chain_ref = refs[3 + 2 * n : 11 + 2 * n]
+    z_ref, k2_ref, s_ref, top_ref, t_ref = refs[11 + 2 * n : 16 + 2 * n]
+    slots = []
+    if n:
+        place = Place()
+        greet(place)
+        slots = schedule(gather_parts(place, cuts, shards, wholes, *refs[16 + 2 * n :]), 0)
+
+    def advance():
+        if slots:
+            for step in slots.pop(0):
+                step()
+
+    advance()
     count = slot // ROWS
     marks = ROWS // 16
     scale = HEAD ** -0.25
@@ -125,16 +156,16 @@
         row = lax.broadcasted_iota(jnp.int32, (ROWS, 1), 0) + i * ROWS
         valid = (row < length).astype(F32)
         few = pl.ds(pl.multiple_of(i * marks, marks), marks)
-        q = q_ref[rows, :] * (valid * scale)
+        q = picked(qkv_ref, rows, 0, wide, parts) * (valid * scale)
         high, low = halves(q)
         qh_ref[rows, :] = high
         small_ref[0, few, :] = mm(avg, high) + mm(avg, low)
-        k = k_ref[rows, :] * (valid * scale)
+        k = picked(qkv_ref, rows, 1, wide, parts) * (valid * scale)
         high, low = halves(k)
         kh_ref[rows, :] = high
         small_ref[1, few, :] = mm(avg, high) + mm(avg, low)
         vp_ref[pl.ds(pl.multiple_of(i * ROWS + EDGE, EDGE), ROWS), :] = (
-            v_ref[rows, :] * valid
+            picked(qkv_ref, rows, 2, wide, parts) * valid
         ).astype(BF)
         return carry
 
@@ -152,6 +183,8 @@
         k2_ref[g] = k2
         small_ref[2, :, at] = gather_up(k2)
         z_ref[g] = jnp.transpose(k2) / top
+
+    advance()
 
     def newton(step, carry):
         for g in range(groups):
@@ -169,7 +202,9 @@
             z_ref[g] = 0.25 * mm3(zs, halves(t3))
         return carry
 
-    lax.fori_loop(0, STEPS, newton, 0)
+    lax.fori_loop(0, STEPS // 2, newton, 0)
+    advance()
+    lax.fori_loop(STEPS // 2, STEPS, newton, 0)
 
     for g in range(groups):
         at = lanes_of(g)
@@ -229,13 +264,32 @@
             return carry
 
         lax.fori_loop(0, count, mix, 0)
-
-
-def attn_bwd_kernel(slot, groups, len_ref, g_ref, qh_ref, kh_ref, vp_ref, k1_ref, k3_ref,
-                    small_ref, chain_ref, flip_ref,
-                    dqkv_ref, conv_ref,
-                    gp_ref, da1_ref, da3_ref, dk_ref, dz_ref, k2_ref,
-                    dql_ref, dkl_ref, t_ref, acc_ref):
+        if g != 1:
+            advance()
+
+    while slots:
+        advance()
+
+
+def attn_bwd_kernel(slot, groups, parts, cuts, *refs):
+    n = 0 if cuts is None else max(c[0] for c in cuts) + 1
+    len_ref, g_ref, qh_ref, kh_ref, vp_ref, k1_ref, k3_ref, small_ref, chain_ref, flip_ref = refs[:10]
+    fulls, outs = refs[10 : 10 + n], refs[10 + n : 10 + 2 * n]
+    dqkv_ref, conv_ref = refs[10 + 2 * n : 12 + 2 * n]
+    (gp_ref, da1_ref, da3_ref, dk_ref, dz_ref, k2_ref,
+     dql_ref, dkl_ref, t_ref, acc_ref) = refs[12 + 2 * n : 22 + 2 * n]
+    slots = []
+    if n:
+        place = Place()
+        greet(place)
+        slots = schedule(scatter_parts(place, cuts, fulls, outs, refs[22 + 2 * n :]), 0)
+
+    def advance():
+        if slots:
+            for step in slots.pop(0):
+                step()
+
+    advance()
     count = slot // ROWS
     marks = ROWS // 16
     scale = HEAD ** -0.25
@@ -289,7 +343,7 @@
             da3_ref[rows, at] = (k3.astype(F32) * (dk3 - total)).astype(BF)
             window = pl.ds(pl.multiple_of(i * ROWS, ROWS), WINDOW)
             dv = mm(k3, dbb) + diagonal_lanes(mm(t_ref[...], gp_ref[window, at]))
-            dqkv_ref[rows, 2 * wide + g * WIDE : 2 * wide + (g + 1) * WIDE] = (dv * valid).astype(BF)
+            put(dqkv_ref, rows, 2, wide, parts, g * WIDE, (dv * valid).astype(BF))
             grad = g_ref[rows, at]
             split = jnp.concatenate(
                 [jnp.where(col == h, grad, jnp.zeros_like(grad)) for h in range(PACK)], axis=0
@@ -305,6 +359,8 @@
         dql_ref[g] = jnp.where(mask, mm(da3_ref[:, at], kh_ref[:, at], TN), 0.0)
         dk_ref[g] = jnp.zeros((WIDE, WIDE), F32)
         k2_ref[g] = spread(small_ref[2, :, at], mask)
+        if g != 1:
+            advance()
 
     def newton(back, carry):
         step = STEPS - 1 - back
@@ -327,7 +383,10 @@
             dz_ref[g] = mm3(t3s, dzs) + mm3(dps, halves(k2_ref[g]))
         return carry
 
-    lax.fori_loop(0, STEPS, newton, 0)
+    lax.fori_loop(0, STEPS // 2, newton, 0)
+    advance()
+    lax.fori_loop(STEPS // 2, STEPS, newton, 0)
+    advance()
 
     for g in range(groups):
         at = lanes_of(g)
@@ -358,11 +417,14 @@
             valid = jnp.where(row < length, scale, 0.0)
             dq = mm(da1_ref[rows, at], klb) + mm(back, dql_ref[g, few, :].astype(BF))
             dk = mm(da3_ref[rows, at], qlb) + mm(back, dkl_ref[g, few, :].astype(BF))
-            dqkv_ref[rows, g * WIDE : (g + 1) * WIDE] = (dq * valid).astype(BF)
-            dqkv_ref[rows, wide + g * WIDE : wide + (g + 1) * WIDE] = (dk * valid).astype(BF)
+            put(dqkv_ref, rows, 0, wide, parts, g * WIDE, (dq * valid).astype(BF))
+            put(dqkv_ref, rows, 1, wide, parts, g * WIDE, (dk * valid).astype(BF))
             return carry
 
         lax.fori_loop(0, count, third, 0)
+
+    while slots:
+        advance()
 
 
 VM = pl.BlockSpec(memory_space=pltpu.VMEM)
@@ -370,13 +432,16 @@
 LIMIT = 60 * 1024 * 1024
 
 
-def attn_fwd(length, q, k, v, taps):
-    slot, wide = q.shape
+def attn_fwd(length, qkv, taps, parts, shards=(), cuts=None, collective_id=1):
+    slot, wide = qkv.shape[0], qkv.shape[1] // 3
     groups = wide // WIDE
     shape = jax.ShapeDtypeStruct
-    return pl.pallas_call(
-        partial(attn_fwd_kernel, slot, groups),
-        out_shape=(
+    talks = dict(collective_id=collective_id, has_side_effects=True) if shards else {}
+    n = len(shards)
+    outs = pl.pallas_call(
+        partial(attn_fwd_kernel, slot, groups, parts, cuts),
+        out_shape=gather_shapes(shards)
+        + (
             shape((slot, wide), BF),
             shape((slot, wide), BF),
             shape((slot, wide), BF),
@@ -386,29 +451,36 @@
             shape((6, MARKS, wide), F32),
             shape((STEPS, KEPT, MARKS, wide), F32),
         ),
-        in_specs=[SM, VM, VM, VM, VM],
-        out_specs=[VM] * 8,
+        in_specs=[SM, VM, VM] + [VM] * n,
+        out_specs=[ANY] * n + [VM] * 8,
         scratch_shapes=[
             pltpu.VMEM((groups, WIDE, WIDE), F32),
             pltpu.VMEM((groups, WIDE, WIDE), F32),
             pltpu.VMEM((slot, WIDE), F32),
             pltpu.VMEM((8, WIDE), F32),
             pltpu.VMEM((PACK * ROWS, WINDOW), BF),
-        ],
-        compiler_params=pltpu.CompilerParams(vmem_limit_bytes=LIMIT),
+        ]
+        + (gather_scratch(cuts) if n else []),
+        compiler_params=pltpu.CompilerParams(vmem_limit_bytes=LIMIT, **talks),
         name="attn_fwd",
-    )(length, q, k, v, taps)
-
-
-def attn_bwd(length, g, qh, kh, vp, k1, k3, small, chain, flip):
+    )(length, qkv, taps, *shards)
+    return outs[:n], outs[n:]
+
+
+def attn_bwd(length, g, saved, flip, parts, fulls=(), cuts=None, collective_id=2):
     slot, wide = g.shape
     groups = wide // WIDE
     shape = jax.ShapeDtypeStruct
-    return pl.pallas_call(
-        partial(attn_bwd_kernel, slot, groups),
-        out_shape=(shape((slot, 3 * wide), BF), shape((16, 256), F32)),
-        in_specs=[SM] + [VM] * 9,
-        out_specs=[VM] * 2,
+    talks = dict(collective_id=collective_id, has_side_effects=True) if fulls else {}
+    n = len(fulls)
+    rows = fulls[0].shape[0] // 16 if n else 0
+    fulls = [f.reshape(2, 2, 2, 2, rows, f.shape[1]) for f in fulls]
+    outs = pl.pallas_call(
+        partial(attn_bwd_kernel, slot, groups, parts, cuts),
+        out_shape=tuple(shape((rows, f.shape[-1] // 2), F32) for f in fulls)
+        + (shape((slot, 3 * wide), BF), shape((16, 256), F32)),
+        in_specs=[SM] + [VM] * 9 + [ANY] * n,
+        out_specs=[VM] * (n + 2),
         scratch_shapes=[
             pltpu.VMEM((slot + 2 * EDGE, wide), BF),
             pltpu.VMEM((slot, wide), BF),
@@ -420,10 +492,355 @@
             pltpu.VMEM((groups, WIDE, WIDE), F32),
             pltpu.VMEM((PACK * ROWS, WINDOW), BF),
             pltpu.VMEM((PACK * ROWS, 256), F32),
-        ],
-        compiler_params=pltpu.CompilerParams(vmem_limit_bytes=LIMIT),
+        ]
+        + (all_scatter_scratch(cuts, rows) if n else []),
+        compiler_params=pltpu.CompilerParams(vmem_limit_bytes=LIMIT, **talks),
         name="attn_bwd",
-    )(length, g, qh, kh, vp, k1, k3, small, chain, flip)
+    )(length, g, *saved, flip, *fulls)
+    return outs[:n], outs[n], outs[n + 1]
+MESH = pl.DeviceIdType.MESH
+WAYS = ("zh", "zl", "y", "x", "c")
+COPIES = 11
+STAGES = 6
+
+
+class Place:
+    def __init__(self):
+        dp = lax.axis_index("dp")
+        self.x = lax.axis_index("tensor")
+        self.zh, self.zl = dp // 8, (dp // 4) % 2
+        self.y, self.c = (dp // 2) % 2, dp % 2
+
+    def at(self, way):
+        spot = {w: getattr(self, w) for w in WAYS}
+        spot[way] = 1 - spot[way]
+        return {
+            "dp": spot["zh"] * 8 + spot["zl"] * 4 + spot["y"] * 2 + spot["c"],
+            "tensor": spot["x"],
+        }
+
+
+def greet(place):
+    barrier = pltpu.get_barrier_semaphore()
+    for way in WAYS:
+        pl.semaphore_signal(barrier, inc=1, device_id=place.at(way), device_id_type=MESH)
+    pl.semaphore_wait(barrier, len(WAYS))
+
+
+class Mover:
+    def __init__(self, place, send, recv, base):
+        self.place, self.send, self.recv, self.base = place, send, recv, base
+        self.started = []
+
+    def copy(self, index, src, dst, way):
+        return pltpu.make_async_remote_copy(
+            src_ref=src, dst_ref=dst,
+            send_sem=self.send.at[self.base + index], recv_sem=self.recv.at[self.base + index],
+            device_id=self.place.at(way), device_id_type=MESH,
+        )
+
+    def push(self, index, src, dst, way):
+        copy = self.copy(index, src, dst, way)
+        copy.start()
+        self.started.append(copy)
+
+    def arrive(self, index, ref, way):
+        self.copy(index, ref, ref, way).wait_recv()
+
+    def drain(self):
+        for copy in self.started:
+            copy.wait_send()
+
+
+class Gather(Mover):
+    def __init__(self, place, shard, whole, lane, width, order, send, recv, base, local):
+        super().__init__(place, send, recv, base)
+        self.shard, self.whole, self.local = shard.at[:, pl.ds(lane, width)], whole, local
+        self.lane, self.width, self.order = lane, width, order
+
+    def view(self, zh, zl, y, c, x):
+        half = self.whole.shape[-1] // 2
+        lanes = pl.ds(pl.multiple_of(x * half + self.lane, 128), self.width)
+        return self.whole.at[zh, zl, y, c, :, lanes]
+
+    def steps(self, c):
+        p, every = self.place, slice(None)
+        yield "zh", [self.view(p.zh, p.zl, p.y, c, p.x)], [self.view(1 - p.zh, p.zl, p.y, c, p.x)]
+        yield "zl", [self.view(every, p.zl, p.y, c, p.x)], [self.view(every, 1 - p.zl, p.y, c, p.x)]
+        if self.order == "yx":
+            yield "y", [self.view(every, every, p.y, c, p.x)], [self.view(every, every, 1 - p.y, c, p.x)]
+            yield "x", [self.view(every, every, every, c, p.x)], [self.view(every, every, every, c, 1 - p.x)]
+        else:
+            yield "x", [self.view(every, every, p.y, c, p.x)], [self.view(every, every, p.y, c, 1 - p.x)]
+            yield (
+                "y",
+                [self.view(every, every, p.y, c, x) for x in (0, 1)],
+                [self.view(every, every, 1 - p.y, c, x) for x in (0, 1)],
+            )
+
+    def run(self, stage):
+        p = self.place
+        here = self.view(p.zh, p.zl, p.y, p.c, p.x)
+        if stage == 0:
+            self.mine, self.other = list(self.steps(p.c)), list(self.steps(1 - p.c))
+            self.push(0, self.shard, here, "zh")
+            self.push(5, self.shard, here, "c")
+            self.own = pltpu.make_async_copy(self.shard, here, self.local)
+            self.own.start()
+        elif stage < 5:
+            way, _, landed = self.mine[stage - 1]
+            for i, ref in enumerate(landed):
+                self.arrive(stage - 1 + i, ref, way)
+            if stage == 1:
+                self.own.wait()
+            if stage < 4:
+                way, outgoing, _ = self.mine[stage]
+                for i, ref in enumerate(outgoing):
+                    self.push(stage + i, ref, ref, way)
+            for i, ref in enumerate(landed):
+                self.push(5 + stage + i, ref, ref, "c")
+        else:
+            self.arrive(5, self.view(p.zh, p.zl, p.y, 1 - p.c, p.x), "c")
+            for k in range(4):
+                for i, ref in enumerate(self.other[k][2]):
+                    self.arrive(6 + k + i, ref, "c")
+            self.drain()
+
+
+class Scatter(Mover):
+    def __init__(self, place, full, lane, width, order, out, bufs, send, recv, base, local):
+        super().__init__(place, send, recv, base)
+        self.full, self.lane, self.width, self.order = full, lane, width, order
+        self.out, self.local = out, local
+        self.sums, self.in_c, self.in_1, self.in_2, self.in_l, self.in_h = bufs
+
+    def lanes(self, x):
+        half = self.full.shape[-1] // 2
+        return pl.ds(x * half + self.lane, self.width)
+
+    def add(self, target, landed):
+        lead = landed.shape[:-2]
+        total = 1
+        for n in lead:
+            total *= n
+        flat_dims = lead
+
+        def one(i, carry):
+            index = []
+            for n in reversed(flat_dims):
+                index.append(i % n)
+                i = i // n
+            index = tuple(reversed(index))
+            target[index] = target[index] + landed[index]
+            return carry
+
+        if total == 1:
+            one(0, 0)
+        else:
+            lax.fori_loop(0, total, one, 0)
+
+    def run(self, stage):
+        p, every = self.place, slice(None)
+        if stage == 0:
+            self.loads = []
+            for x in (0, 1):
+                self.push(x, self.full.at[:, :, :, 1 - p.c, :, self.lanes(x)], self.in_c.at[x], "c")
+                load = pltpu.make_async_copy(
+                    self.full.at[:, :, :, p.c, :, self.lanes(x)], self.sums.at[x], self.local.at[x]
+                )
+                load.start()
+                self.loads.append(load)
+            return
+        if stage == 1:
+            for x in (0, 1):
+                self.arrive(x, self.in_c.at[x], "c")
+                self.loads[x].wait()
+            self.add(self.sums, self.in_c)
+            if self.order == "xy":
+                self.push(2, self.sums.at[1 - p.x], self.in_1.at[...], "x")
+            else:
+                for x in (0, 1):
+                    self.push(2 + x, self.sums.at[x, :, :, 1 - p.y], self.in_1.at[x], "y")
+        elif stage == 2:
+            if self.order == "xy":
+                self.arrive(2, self.in_1, "x")
+                self.add(self.sums.at[p.x], self.in_1)
+                self.push(4, self.sums.at[p.x, :, :, 1 - p.y], self.in_2, "y")
+            else:
+                for x in (0, 1):
+                    self.arrive(2 + x, self.in_1.at[x], "y")
+                    self.add(self.sums.at[x, :, :, p.y], self.in_1.at[x])
+                self.push(4, self.sums.at[1 - p.x, :, :, p.y], self.in_2, "x")
+        elif stage == 3:
+            self.arrive(4, self.in_2, "y" if self.order == "xy" else "x")
+            self.add(self.sums.at[p.x, :, :, p.y], self.in_2)
+            self.push(5, self.sums.at[p.x, :, 1 - p.zl, p.y], self.in_l, "zl")
+        elif stage == 4:
+            self.arrive(5, self.in_l, "zl")
+            self.add(self.sums.at[p.x, :, p.zl, p.y], self.in_l)
+            self.push(6, self.sums.at[p.x, 1 - p.zh, p.zl, p.y], self.in_h, "zh")
+        else:
+            self.arrive(6, self.in_h, "zh")
+            self.out[:, self.lane : self.lane + self.width] = (
+                self.sums[p.x, p.zh, p.zl, p.y].astype(F32) + self.in_h[...].astype(F32)
+            )
+            self.drain()
+
+
+def scatter_scratch(rows, width, order):
+    first = (2, 2, 2) if order == "xy" else (2, 2, 2)
+    return [
+        pltpu.VMEM((2, 2, 2, 2, rows, width), BF),
+        pltpu.VMEM((2, 2, 2, 2, rows, width), BF),
+        pltpu.VMEM(first + (rows, width), BF),
+        pltpu.VMEM((2, 2, rows, width), BF),
+        pltpu.VMEM((2, rows, width), BF),
+        pltpu.VMEM((rows, width), BF),
+    ]
+
+
+class Total(Mover):
+    def __init__(self, place, block, out, sums, landed, send, recv, base):
+        super().__init__(place, send, recv, base)
+        self.block, self.out, self.sums, self.landed = block, out, sums, landed
+
+    def run(self, stage):
+        if stage == 0:
+            self.sums[0] = self.block[...]
+        else:
+            self.arrive(stage - 1, self.landed.at[stage - 1], WAYS[stage - 1])
+            self.sums[stage] = self.sums[stage - 1] + self.landed[stage - 1]
+        if stage < 5:
+            self.push(stage, self.sums.at[stage], self.landed.at[stage], WAYS[stage])
+        else:
+            self.out[...] = self.sums[5]
+            self.drain()
+
+
+def schedule(parts, lag=1):
+    slots = [[] for _ in range(STAGES + lag * (len(parts) - 1))]
+    for i, part in enumerate(parts):
+        for stage in range(STAGES):
+            slots[stage + lag * i].append((part, stage))
+    return [[partial(part.run, stage) for part, stage in slot] for slot in slots]
+
+
+def cut(widths, piece):
+    out = []
+    for i, width in enumerate(widths):
+        lane = 0
+        while lane < width:
+            take = min(piece, width - lane)
+            out.append((i, lane, take, ("yx", "xy")[len(out) % 2]))
+            lane += take
+    return tuple(out)
+
+
+def gather_parts(place, cuts, shards, wholes, send, recv, local):
+    return [
+        Gather(place, shards[i], wholes[i], lane, width, order, send, recv, COPIES * n, local.at[n])
+        for n, (i, lane, width, order) in enumerate(cuts)
+    ]
+
+
+def gather_scratch(cuts):
+    n = len(cuts)
+    return [
+        pltpu.SemaphoreType.DMA((COPIES * n,)),
+        pltpu.SemaphoreType.DMA((COPIES * n,)),
+        pltpu.SemaphoreType.DMA((n,)),
+    ]
+
+
+def gather_shapes(shards):
+    return tuple(
+        jax.ShapeDtypeStruct((2, 2, 2, 2, s.shape[0], 2 * s.shape[1]), s.dtype) for s in shards
+    )
+
+
+def gather_kernel(cuts, lag, n, *refs):
+    shards, wholes = refs[:n], refs[n : 2 * n]
+    place = Place()
+    greet(place)
+    parts = gather_parts(place, cuts, shards, wholes, *refs[2 * n :])
+    for slot in schedule(parts, lag):
+        for step in slot:
+            step()
+
+
+def gather_call(shards, cuts, lag, collective_id):
+    n = len(shards)
+    return pl.pallas_call(
+        partial(gather_kernel, cuts, lag, n),
+        out_shape=gather_shapes(shards),
+        in_specs=[VM] * n,
+        out_specs=[ANY] * n,
+        scratch_shapes=gather_scratch(cuts),
+        compiler_params=pltpu.CompilerParams(
+            collective_id=collective_id, has_side_effects=True, vmem_limit_bytes=LIMIT
+        ),
+        name=f"gather_{collective_id}",
+    )(*shards)
+
+
+SUM_COPIES = 7
+
+
+def scatter_parts(place, cuts, fulls, outs, refs):
+    send, recv, local = refs[-3:]
+    return [
+        Scatter(place, fulls[i], lane, width, order, outs[i], refs[6 * n : 6 * n + 6],
+                send, recv, SUM_COPIES * n, local.at[n])
+        for n, (i, lane, width, order) in enumerate(cuts)
+    ]
+
+
+def all_scatter_scratch(cuts, rows, extra=0):
+    out = []
+    for _, _, width, order in cuts:
+        out += scatter_scratch(rows, width, order)
+    n = len(cuts)
+    return out + [
+        pltpu.SemaphoreType.DMA((SUM_COPIES * n + extra,)),
+        pltpu.SemaphoreType.DMA((SUM_COPIES * n + extra,)),
+        pltpu.SemaphoreType.DMA((n, 2)),
+    ]
+
+
+def scatter_kernel(cuts, lag, n, block_ref, *refs):
+    fulls, outs, sum_ref = refs[:n], refs[n : 2 * n], refs[2 * n]
+    sums, landed = refs[2 * n + 1 : 2 * n + 3]
+    rest = refs[2 * n + 3 :]
+    place = Place()
+    greet(place)
+    parts = scatter_parts(place, cuts, fulls, outs, rest)
+    total = Total(place, block_ref, sum_ref, sums, landed, rest[-3], rest[-2], SUM_COPIES * len(cuts))
+    slots = schedule(parts, lag)
+    for i in range(STAGES):
+        slots[i].append(partial(total.run, i))
+    for slot in slots:
+        for step in slot:
+            step()
+
+
+def scatter_call(block, fulls, cuts, lag, collective_id):
+    n = len(fulls)
+    rows = fulls[0].shape[0] // 16
+    shape = jax.ShapeDtypeStruct
+    fulls = [f.reshape(2, 2, 2, 2, rows, f.shape[1]) for f in fulls]
+    return pl.pallas_call(
+        partial(scatter_kernel, cuts, lag, n),
+        out_shape=tuple(shape((rows, f.shape[-1] // 2), F32) for f in fulls)
+        + (shape(block.shape, F32),),
+        in_specs=[VM] + [ANY] * n,
+        out_specs=[VM] * (n + 1),
+        scratch_shapes=[pltpu.VMEM((6,) + block.shape, F32), pltpu.VMEM((5,) + block.shape, F32)]
+        + all_scatter_scratch(cuts, rows, 5),
+        compiler_params=pltpu.CompilerParams(
+            collective_id=collective_id, has_side_effects=True, vmem_limit_bytes=LIMIT
+        ),
+        name=f"scatter_{collective_id}",
+    )(block, *fulls)
 
 
 D = 768
@@ -460,66 +877,67 @@
     )
 
 
-def gather_weights(pieces):
-    joined = lax.all_gather(jnp.concatenate(pieces, axis=1), BOTH, axis=0, tiled=True)
-    halves_of = lax.axis_size("tensor")
-    joined = joined.reshape(halves_of, D, -1)
-    whole, start = [], 0
+def gather_plain(pieces):
+    sizes = lax.axis_size("tensor"), lax.axis_size("dp")
+    out = []
     for piece in pieces:
-        width = piece.shape[1]
-        part = joined[:, :, start : start + width]
-        whole.append(part.transpose(1, 0, 2).reshape(D, halves_of * width))
-        start += width
-    return whole
-
-
-def scatter_grads(fulls):
-    halves_of = lax.axis_size("tensor")
-    stacked = jnp.concatenate(
-        [
-            jnp.concatenate(
-                [
-                    full[:, t * full.shape[1] // halves_of : (t + 1) * full.shape[1] // halves_of]
-                    for t in range(halves_of)
-                ],
-                axis=0,
-            )
-            for full in fulls
-        ],
-        axis=1,
-    )
-    mine = lax.psum_scatter(stacked, BOTH, scatter_dimension=0, tiled=True)
-    out, start = [], 0
+        joined = lax.all_gather(piece, BOTH, axis=0, tiled=True)
+        joined = joined.reshape(sizes[0], sizes[1] * piece.shape[0], piece.shape[1])
+        out.append(joined.transpose(1, 0, 2).reshape(joined.shape[1], -1))
+    return out
+
+
+def scatter_plain(fulls):
+    parts = lax.axis_size("tensor")
+    out = []
     for full in fulls:
-        width = full.shape[1] // halves_of
-        out.append(mine[:, start : start + width].astype(F32))
-        start += width
+        stacked = full.reshape(full.shape[0], parts, -1).transpose(1, 0, 2).reshape(-1, full.shape[1] // parts)
+        out.append(lax.psum_scatter(stacked, BOTH, scatter_dimension=0, tiled=True).astype(F32))
     return out
 
 
-def per_device(x_in, lengths, cotangent, w_query, w_key, w_value, w_out, w_in, w_down,
+def per_device(own, x_in, lengths, cotangent, w_query, w_key, w_value, w_out, w_in, w_down,
                conv_weight, ln1_gain, ln1_bias, ln2_gain, ln2_bias):
     tensor_index = lax.axis_index("tensor")
     slot = x_in.shape[0]
-    halves_of = lax.axis_size("tensor")
+    parts = lax.axis_size("tensor")
     length = lax.dynamic_slice_in_dim(lengths, tensor_index, 1)
     valid = (jnp.arange(slot, dtype=jnp.int32) < length[0]).astype(F32)[:, None]
 
-    query_w, key_w, value_w = gather_weights((w_query, w_key, w_value))
-    out_w, in_w, down_w = gather_weights((w_out.T, w_in, w_down.T))
-    gains = lax.all_gather(
-        jnp.stack([ln1_gain, ln1_bias, ln2_gain, ln2_bias]), ("dp", "tensor"), axis=1, tiled=True
-    )
+    first = jnp.concatenate([w_query, w_key, w_value], axis=1)
+    later = (w_out.T, w_in, w_down.T)
+    few, own_heads, count = ln1_gain.shape[0], conv_weight.shape[0], conv_weight.shape[1]
+    if own:
+        vectors = jnp.pad(
+            jnp.stack([ln1_gain, ln1_bias, ln2_gain, ln2_bias]), ((0, 4), (0, 128 - few))
+        )
+        block = jnp.concatenate(
+            [vectors, jnp.pad(conv_weight, ((0, 8 - own_heads), (0, 128 - count)))], axis=0
+        )
+        qkv_w, blocks = gather_call([first, block], FIRST_CUTS, 0, 0)
+        qkv_w = qkv_w.reshape(D, -1)
+        blocks = blocks.reshape(lax.axis_size("dp"), 16, parts, 128)
+        gains = blocks[:, :4, :, :few].transpose(1, 0, 2, 3).reshape(4, D)
+        taps = blocks[0, 8 : 8 + own_heads, :, :count].transpose(1, 0, 2).reshape(-1, count)
+    else:
+        (qkv_w,) = gather_plain([first])
+        gains = lax.all_gather(
+            jnp.stack([ln1_gain, ln1_bias, ln2_gain, ln2_bias]), ("dp", "tensor"), axis=1, tiled=True
+        )
+        taps = lax.all_gather(conv_weight, "tensor", axis=0, tiled=True)
     gain_one, bias_one, gain_two, bias_two = gains[0], gains[1], gains[2], gains[3]
-    taps = lax.all_gather(conv_weight, "tensor", axis=0, tiled=True)
-    heads, count = taps.shape
+    heads = own_heads * parts
     room = ((0, 16 - heads), (0, 256 - count))
 
     tokens = x_in.astype(F32)
-    queries, keys_all, values_all = dense(x_in, query_w), dense(x_in, key_w), dense(x_in, value_w)
-    ctx, qh, kh, vp, k1, k3, small, chain = attn_fwd(
-        length, queries, keys_all, values_all, jnp.pad(taps, room)
-    )
+    qkv = dense(x_in, qkv_w)
+    if own:
+        wholes, saved = attn_fwd(length, qkv, jnp.pad(taps, room), parts, later, LATER_CUTS)
+        out_w, in_w, down_w = (w.reshape(D, -1) for w in wholes)
+    else:
+        _, saved = attn_fwd(length, qkv, jnp.pad(taps, room), parts)
+        out_w, in_w, down_w = gather_plain(later)
+    ctx, saved = saved[0], saved[1:]
     attn_branch = cols_sum(ctx, out_w)
     normal_one, inverse_one = norm_parts(tokens + attn_branch)
     hidden = (normal_one * gain_one + bias_one).astype(BF)
@@ -541,47 +959,59 @@
     d_attn = d_res1.astype(BF)
     grad_out = rows_sum(d_attn, ctx)
     d_ctx = dense(d_attn, out_w).astype(BF)
-    early = scatter_grads([grad_out.astype(BF), grad_in.astype(BF), grad_down.astype(BF)])
-    d_qkv, conv_rows = attn_bwd(
-        length, d_ctx, qh, kh, vp, k1, k3, small, chain, jnp.pad(taps[:, ::-1], room)
-    )
-    qkv_w = jnp.concatenate([query_w, key_w, value_w], axis=1)
+    fulls = [grad_out.astype(BF), grad_in.astype(BF), grad_down.astype(BF)]
+    flip = jnp.pad(taps[:, ::-1], room)
+    if own:
+        early, d_qkv, conv_rows = attn_bwd(length, d_ctx, saved, flip, parts, fulls, LATER_CUTS)
+    else:
+        _, d_qkv, conv_rows = attn_bwd(length, d_ctx, saved, flip, parts)
+        early = scatter_plain(fulls)
+    grad_qkv = rows_sum(x_in, d_qkv).astype(BF)
     input_grad = (d_res1 + cols_sum(d_qkv, qkv_w)).astype(BF)
-    grad_qkv = rows_sum(x_in, d_qkv).astype(BF)
-    late = scatter_grads([grad_qkv[:, :D], grad_qkv[:, D : 2 * D], grad_qkv[:, 2 * D :]])
 
     def total(branch):
         return jnp.sum(valid * branch * branch)
 
-    summed = lax.psum(
-        jnp.concatenate(
-            [
-                grad_gain_one, grad_bias_one, grad_gain_two, grad_bias_two,
-                conv_rows[:heads, ROWS - 1 : ROWS - 1 + count].reshape(-1),
-                jnp.stack([total(tokens), total(attn_branch), total(ffn_branch), jnp.sum(valid)]),
-            ]
-        ),
-        ("dp", "tensor"),
+    sums = jnp.concatenate(
+        [
+            grad_gain_one, grad_bias_one, grad_gain_two, grad_bias_two,
+            conv_rows[:heads, ROWS - 1 : ROWS - 1 + count].reshape(-1),
+            jnp.stack([total(tokens), total(attn_branch), total(ffn_branch), jnp.sum(valid)]),
+        ]
     )
+    if own:
+        late, summed = scatter_call(
+            jnp.pad(sums, (0, 4096 - sums.shape[0])).reshape(32, 128), [grad_qkv], LAST_CUTS, 0, 3
+        )
+        summed = summed.reshape(-1)
+    else:
+        (late,) = scatter_plain([grad_qkv])
+        summed = lax.psum(sums, ("dp", "tensor"))
     share = D // lax.axis_size(("dp", "tensor"))
     start_at = lax.axis_index(("dp", "tensor")) * share
     vectors = lax.dynamic_slice_in_dim(summed[: 4 * D].reshape(4, D), start_at, share, 1)
     conv_all = summed[4 * D : 4 * D + heads * count].reshape(heads, count)
-    own_heads = heads // halves_of
     conv_grad = lax.dynamic_slice_in_dim(conv_all, tensor_index * own_heads, own_heads, 0)
     sums = summed[4 * D + heads * count :]
     stats = jnp.sqrt(sums[:3] / (sums[3] * D))
+    width = late.shape[1] // 3
     return (
-        output, input_grad, late[0], late[1], late[2], early[0].T, early[1], early[2].T,
+        output, input_grad, late[:, :width], late[:, width : 2 * width], late[:, 2 * width :], early[0].T, early[1], early[2].T,
         conv_grad, vectors[0], vectors[1], vectors[2], vectors[3], stats,
     )
 
 
+FIRST_CUTS = ((0, 0, 640, "yx"), (0, 640, 512, "xy"), (1, 0, 128, "yx"))
+LATER_CUTS = ((1, 0, 1536, "xy"), (2, 0, 1536, "yx"), (0, 0, 384, "xy"))
+LAST_CUTS = ((0, 0, 640, "yx"), (0, 640, 512, "xy"))
+
+
 def solution(mesh):
+    own = mesh.shape["dp"] == 16 and mesh.shape["tensor"] == 2
     rows, both = P(("dp", "tensor"), None), P(("dp", "tensor"))
     split, crossed = P("dp", "tensor"), P("tensor", "dp")
     return jax.shard_map(
-        per_device,
+        partial(per_device, own),
         mesh=mesh,
         in_specs=(rows, P("dp"), rows, split, split, split, crossed, split, crossed,
                   P("tensor", None), both, both, both, both),

time: 616 us -> 405 us (0.66)
  Pallas kernels: 112 us -> 259 us
  waiting for transfers between devices: 120 us -> 0 us
  blocking collectives: 113 us -> 0 us
  other arithmetic: 94 us -> 15.7 us
  local copies, waits for them, and re-layouts: 58.4 us -> 26 us
  between operations: 15.2 us -> 1.9 us
    pallas_call x2 -> x4, Pallas kernels: 112 us -> 259 us  [the longest x1 92.2 us: attn_bwd(): pl.pallas_call(partial(attn_bwd_kernel, slot, groups, parts, cuts), out_s...]
    reduce_scatter x2 -> x0, waiting for transfers between devices: 120 us -> none  [scatter_grads(): mine = lax.psum_scatter(stacked, BOTH, scatter_dimension=0, tiled=True)]
    concatenate x4 -> x2, other arithmetic: 77.1 us -> 2.75 us  [the longest x1 1.46 us: per_device(): first = jnp.concatenate([w_query, w_key, w_value], axis=1)]
    all_gather x2 -> x0, blocking collectives: 74 us -> none  [the longest x1 68.5 us: per_device(): lax.all_gather(jnp.stack([ln1_gain, ln1_bias, ln2_gain, ln2_bias]), ('dp'...]
    psum x1 -> x0, blocking collectives: 39.1 us -> none  [per_device(): lax.psum(jnp.concatenate([grad_gain_one, grad_bias_one, grad_gain_two, gr...]
    transpose x9 -> x1, local copies, waits for them, and re-layouts: 30.3 us -> 0.01 us  [per_device(): gains = blocks[:, :4, :, :few].transpose(1, 0, 2, 3).reshape(4, D)]
    dot_general x4, matrix products: 21.7 us -> 31.1 us  [rows_sum(): lax.dot_general(left_op, right_op, (TN, ((), ())), preferred_element_type...]
    unnamed x74 -> x54, local copies, waits for them, and re-layouts: 16.6 us -> 13 us
  transfers between devices with their start and end apart: 4 -> 0, of which waited for: 1 -> 0; matrix products, arithmetic and copies ran while one was open for 18% -> 0% of each run, Pallas kernels for 9% -> 0%
where the time goes in v2:
time: 405 us; the launch traced here: 401 us
  Pallas kernels  259 us (64%)
  matrix products  97.9 us (24%)
  local copies, waits for them, and re-layouts  26 us (6%)
  other arithmetic  15.7 us (4%)
    pallas_call x1, Pallas kernels, attn_bwd(): pl.pallas_call(partial(attn_bwd_kernel, slot, groups, parts, cuts), out_s...  92.2 us
    pallas_call x1, Pallas kernels, attn_fwd(): pl.pallas_call(partial(attn_fwd_kernel, slot, groups, parts, cuts), out_s...  91.1 us
    pallas_call x1, Pallas kernels, scatter_call(): pl.pallas_call(partial(scatter_kernel, cuts, lag, n), out_shape=tuple((sh...  38 us
    pallas_call x1, Pallas kernels, gather_call(): pl.pallas_call(partial(gather_kernel, cuts, lag, n), out_shape=gather_sha...  37.7 us
    dot_general x4, matrix products, dense(): return jnp.dot(left_op, right_op, preferred_element_type=F32)  36.2 us
    dot_general x4, matrix products, rows_sum(): lax.dot_general(left_op, right_op, (TN, ((), ())), preferred_element_type...  31.1 us
    dot_general x4, matrix products, cols_sum(): lax.dot_general(left_op, right_op, (NT, ((), ())), preferred_element_type...  30.6 us
    unnamed x54, local copies, waits for them, and re-layouts  13 us

profile of v2, /device:TPU:0, one launch (start us, length us, event | category | flops | bytes accessed | tf_op | source)
XLA Modules:
  0.0 400.7 jit_solution(14829501275369802428)
XLA Ops:
  5.4 37.7 %gather_0.1 = (bf16[2,2,2,2,48,2304]{5,4,3,2,1,0:T(8,128)(2,1)}, f32[2,2,2,2,16,256]{5,4,3,2,1,0:T(8,128)}) custom-call(bf16[48,1152]{1,0:T(8,128)(2,1)} %pad_maximum_fusion.refs_0_, f32[16,128]{1,0:T(8,128)} %select_maximum_fusion.refs_1_), custom_call_target="tpu_custom_call" | custom-call | tf_op jit(solution)/shard_map/gather_0/pallas_call | solution.py:773
  44.8 9.9 %convolution_bitcast_fusion.refs_1_ = f32[1024,2304]{1,0:T(8,128)} fusion(bf16[1024,768]{1,0:T(8,128)(2,1)} %param.14, bf16[768,2304]{1,0:T(8,128)(2,1)} %bitcast.98), kind=kOutput, calls=%fused_computation.9 | convolution fusion | flops 3623878656 | bytes 14548992 | tf_op jit(solution)/shard_map/dot_general | solution.py:859
  54.7 91.1 %attn_fwd.1 = (bf16[2,2,2,2,48,768]{5,4,3,2,1,0:T(8,128)(2,1)}, bf16[2,2,2,2,48,3072]{5,4,3,2,1,0:T(8,128)(2,1)}, bf16[2,2,2,2,48,3072]{5,4,3,2,1,0:T(8,128)(2,1...) custom-call(s32[1]{0:T(128)} %dynamic_slice.9.refs_0_, ...), custom_call_target="tpu_custom_call" | custom-call | tf_op jit(solution)/shard_map/attn_fwd/pallas_call | solution.py:441
  145.9 1.6 copy.36
  147.5 5.3 %fusion.19 = (f32[1024]{0:T(1024)S(1)}, f32[1024,768]{0,1:T(8,128)S(1)}, f32[1024,768]{0,1:T(8,128)}) fusion(bf16[1024,768]{0,1:T(8,128)(2,1)} %copy.36, bf16[1024,768]{1,0:T(8,128)(2,1)} %get-tuple-element.36, bf16[768,768]{1,0:T(8,128)(2,1)} %bitcast.75), kind=kOutput, calls=%fused_computation.77 | convolution fusion | flops 1210317824 | bytes 10620928 | tf_op jit(solution)/shard_map/dot_general | solution.py:855
  153.5 11.7 %multiply_convert_fusion.1 = (bf16[1024,3072]{1,0:T(8,128)(2,1)S(1)}, f32[1024,3072]{1,0:T(8,128)}) fusion(bf16[768,3072]{1,0:T(8,128)(2,1)} %bitcast.90, f32[1024,768]{0,1:T(8,128)S(1)} %get-tuple-element.100, f32[768]{0:T(1024)S(1)} %add.82, f32[768]{0:T(1024)S(1)} %mul.183, f32[1024]{0:T(1024)S(1)} %add_rsqrt_fusion.1, f32[1024]{0:T(1024)S(1)} %broadcast_multiply_fusion.5), kind=kOutput, calls=%fused_computation.7 | convolution fusion | flops 4851499008 | bytes 26753024 | tf_op jit(solution)/shard_map/dot_general | solution.py:859
  165.2 10.2 %fusion.18 = (f32[1024]{0:T(1024)S(1)}, f32[1024,768]{0,1:T(8,128)S(1)}, f32[1024,768]{0,1:T(8,128)}) fusion(bf16[1024,3072]{1,0:T(8,128)(2,1)S(1)} %get-tuple-element.114, bf16[768,3072]{1,0:T(8,128)(2,1)} %bitcast.94, f32[768]{0:T(1024)S(1)} %add.82, f32[768]{0:T(1024)S(1)} %mul.183, f32[1024]{0:T(1024)S(1)} %add_rsqrt_fusion.1, ...), kind=kOutput, calls=%fused_computation.76 | convolution fusion | flops 4838128640 | bytes 20465664 | tf_op jit(solution)/shard_map/dot_general | solution.py:855
  175.4 1.8 copy-done
  178.4 2.6 copy.39
  181.0 7.3 %fusion.7 = (f32[]{:T(128)}, f32[]{:T(128)}, f32[768]{0:T(1024)S(1)}, f32[1024]{0:T(1024)S(1)}, f32[1024]{0:T(1024)S(1)}, /*index=5*/f32[768]{0:T(1024)S(1)}, f32[]{:T(128)}, bf16[1024,768]{0,1:T(8,128)(2,1)}) fusion(f32[1024,768]{0,1:T(8,128)} %get-tuple-element.116, f32[1024]{0:T(1024)S(1)} %fusion.15, f32[1024,768]{0,1:T(8,128)} %get-tuple-element.113, ...), kind=kLoop, calls=%fused_computation.19 | loop fusion | flops 18870780 | bytes 14188556 | tf_op jit(solution)/shard_map/reduce_sum | solution.py:973
  188.4 10.8 %convolution_convert_fusion = bf16[768,3072]{1,0:T(8,128)(2,1)} fusion(bf16[1024,3072]{1,0:T(8,128)(2,1)} %copy-done.15, bf16[1024,768]{0,1:T(8,128)(2,1)S(1)} %copy-done.3, f32[1024,768]{0,1:T(8,128)S(1)} %copy-done.1, f32[1024]{0:T(1024)S(1)} %get-tuple-element.118, f32[1024]{0:T(1024)S(1)} %get-tuple-element.119, f32[1024]{0:T(1024)S(1)} %fusion.15, ...), kind=kOutput, calls=%fused_computation.10 | convolution fusion | flops 4842061824 | bytes 15752192 | tf_op jit(solution)/shard_map/dot_general | solution.py:851
  199.2 11.9 %multiply_convert_fusion = bf16[1024,3072]{1,0:T(8,128)(2,1)} fusion(bf16[768,3072]{1,0:T(8,128)(2,1)S(1)} %bitcast.97, f32[1024,3072]{1,0:T(8,128)S(1)} %bitcast.101, bf16[1024,768]{0,1:T(8,128)(2,1)S(1)} %copy-done.3, f32[1024,768]{0,1:T(8,128)S(1)} %copy-done.1, f32[1024]{0:T(1024)S(1)} %get-tuple-element.118, f32[1024]{0:T(1024)S(1)} %get-tuple-element.119, ...), kind=kOutput, calls=%fused_computation.6 | convolution fusion | flops 4877451264 | bytes 28335104 | tf_op jit(solution)/shard_map/dot_general | solution.py:859
  211.1 10.0 %convolution_convert_fusion.1 = bf16[768,3072]{1,0:T(8,128)(2,1)} fusion(bf16[1024,3072]{1,0:T(8,128)(2,1)} %multiply_convert_fusion, f32[1024,768]{0,1:T(8,128)S(1)} %get-tuple-element.100, f32[768]{0:T(1024)S(1)} %add.82, f32[768]{0:T(1024)S(1)} %mul.183, f32[1024]{0:T(1024)S(1)} %add_rsqrt_fusion.1, f32[1024]{0:T(1024)S(1)} %broadcast_multiply_fusion.5), kind=kOutput, calls=%fused_computation.11 | convolution fusion | flops 4838129664 | bytes 14170112 | tf_op jit(solution)/shard_map/dot_general | solution.py:851
  221.2 6.7 %multiply_reduce_fusion.1 = (f32[768]{0:T(1024)S(1)}, f32[1024]{0:T(1024)S(1)}, f32[1024]{0:T(1024)S(1)}, f32[768]{0:T(1024)S(1)}, f32[1024,768]{0,1:T(8,128)S(1)}) fusion(f32[1024,768]{0,1:T(8,128)S(1)} %get-tuple-element.100, f32[1024]{0:T(1024)S(1)} %add_rsqrt_fusion.1, f32[1024]{0:T(1024)S(1)} %broadcast_multiply_fusion.5, f32[768]{0:T(1024)S(1)} %mul.183, ...), kind=kOutput, calls=%fused_computation.21 | convolution fusion | flops 4846776320 | bytes 22069248 | tf_op jit(solution)/shard_map/dot_general | solution.py:855
  229.4 2.4 convolution_convert_fusion.4
  231.8 2.6 convolution_convert_fusion.3.refs_1_
  235.1 92.2 %attn_bwd.1 = (f32[48,384]{1,0:T(8,128)}, f32[48,1536]{1,0:T(8,128)}, f32[48,1536]{1,0:T(8,128)}, bf16[1024,2304]{1,0:T(8,128)(2,1)}, f32[16,256]{1,0:T(8,128)}) custom-call(s32[1]{0:T(128)} %dynamic_slice.9.refs_0_, bf16[1024,768]{1,0:T(8,128)(2,1)} %convolution_convert_fusion.3.refs_1_, bf16[1024,768]{1,0:T(8,128)(2,1)} %get-tuple-element.40.refs_2_, ...), custom_call_target="tpu_custom_call" | custom-call | tf_op jit(solution)/shard_map/attn_bwd/pallas_call | solution.py:478
  327.3 7.9 %convolution_convert_fusion.2 = bf16[2304,768]{0,1:T(8,128)(2,1)} fusion(bf16[1024,2304]{1,0:T(8,128)(2,1)} %get-tuple-element.47, bf16[1024,768]{1,0:T(8,128)(2,1)S(1)} %copy-done.8), kind=kOutput, calls=%fused_computation.12 | convolution fusion | flops 3625648128 | bytes 9830400 | tf_op jit(solution)/shard_map/dot_general | solution.py:851
  336.8 2.7 concatenate.11
  340.1 38.0 %scatter_3.1 = (f32[48,1152]{1,0:T(8,128)}, f32[32,128]{1,0:T(8,128)}) custom-call(f32[32,128]{1,0:T(8,128)} %pad_bitcast_fusion.block_ref, bf16[2,2,2,2,48,2304]{5,4,3,2,1,0:T(8,128)(2,1)} %bitcast.74), custom_call_target="tpu_custom_call" | custom-call | tf_op jit(solution)/shard_map/scatter_3/pallas_call | solution.py:831
  381.3 1.6 fusion.20
  385.6 8.4 %add_convert_fusion = bf16[1024,768]{0,1:T(8,128)(2,1)} fusion(f32[1024,768]{0,1:T(8,128)S(1)} %copy-done.6, bf16[1024,2304]{1,0:T(8,128)(2,1)} %get-tuple-element.47, bf16[768,2304]{1,0:T(8,128)(2,1)} %bitcast.99), kind=kOutput, calls=%fused_computation.22 | convolution fusion | flops 3625451520 | bytes 12976128 | tf_op jit(solution)/shard_map/dot_general | solution.py:855
  394.1 2.7 copy.43
  396.8 1.6 copy.42
  (92 shorter events, 19.9 us)
Async XLA Ops:
  54.7 91.2 %copy-start.7 = (bf16[1024,768]{1,0:T(8,128)(2,1)S(1)}, bf16[1024,768]{1,0:T(8,128)(2,1)}, u32[]{:S(2)}) copy-start(bf16[1024,768]{1,0:T(8,128)(2,1)} %param.14) | copy-start | bytes 4718596
  165.2 10.2 %copy-start.15 = (bf16[1024,3072]{1,0:T(8,128)(2,1)}, bf16[1024,3072]{1,0:T(8,128)(2,1)S(1)}, u32[]{:S(2)}) copy-start(bf16[1024,3072]{1,0:T(8,128)(2,1)S(1)} %get-tuple-element.114) | copy-start | bytes 18874372
  175.4 1.8 copy-start
  181.0 7.3 %copy-start.1 = (f32[1024,768]{0,1:T(8,128)S(1)}, f32[1024,768]{0,1:T(8,128)}, u32[]{:S(2)}) copy-start(f32[1024,768]{0,1:T(8,128)} %copy-done) | copy-start | bytes 9437188
  181.0 7.3 %copy-start.3 = (bf16[1024,768]{0,1:T(8,128)(2,1)S(1)}, bf16[1024,768]{0,1:T(8,128)(2,1)}, u32[]{:S(2)}) copy-start(bf16[1024,768]{0,1:T(8,128)(2,1)} %copy.39) | copy-start | bytes 4718596
  181.0 18.2 %slice-start.2 = ((s8[4718592]{0:T(1024)(128)(4,1)}), s8[4194304]{0:T(1024)(128)(4,1)S(1)}, s32[]{:S(2)}) async-start(s8[4718592]{0:T(1024)(128)(4,1)} %bitcast.95), calls=%async_computation.2 | async-start | bytes 8388608
  181.0 18.2 %slice-start.4 = ((s8[12582912]{0:T(1024)(128)(4,1)}), s8[4194304]{0:T(1024)(128)(4,1)S(1)}, s32[]{:S(2)}) async-start(s8[12582912]{0:T(1024)(128)(4,1)} %bitcast.100), calls=%async_computation.4 | async-start | bytes 8388608
  188.3 10.8 %slice-start.3 = ((s8[4718592]{0:T(1024)(128)(4,1)}), s8[524288]{0:T(1024)(128)(4,1)S(1)}, s32[]{:S(2)}) async-start(s8[4718592]{0:T(1024)(128)(4,1)} %bitcast.95), calls=%async_computation.3 | async-start | bytes 1048576
  188.3 10.8 %slice-start.5 = ((s8[12582912]{0:T(1024)(128)(4,1)}), s8[4194304]{0:T(1024)(128)(4,1)S(1)}, s32[]{:S(2)}) async-start(s8[12582912]{0:T(1024)(128)(4,1)} %bitcast.100), calls=%async_computation.5 | async-start | bytes 8388608
  188.3 10.8 %slice-start.6 = ((s8[12582912]{0:T(1024)(128)(4,1)}), s8[4194304]{0:T(1024)(128)(4,1)S(1)}, s32[]{:S(2)}) async-start(s8[12582912]{0:T(1024)(128)(4,1)} %bitcast.100), calls=%async_computation.6 | async-start | bytes 8388608
  188.3 32.8 %slice-start = ((s8[4718592]{0:T(1024)(128)(4,1)}), s8[4194304]{0:T(1024)(128)(4,1)S(1)}, s32[]{:S(2)}) async-start(s8[4718592]{0:T(1024)(128)(4,1)} %bitcast.91), calls=%async_computation | async-start | bytes 8388608
  199.2 22.0 %slice-start.1 = ((s8[4718592]{0:T(1024)(128)(4,1)}), s8[524288]{0:T(1024)(128)(4,1)S(1)}, s32[]{:S(2)}) async-start(s8[4718592]{0:T(1024)(128)(4,1)} %bitcast.91), calls=%async_computation.1 | async-start | bytes 1048576
  211.1 10.1 %copy-start.14 = (bf16[1024,3072]{1,0:T(8,128)(2,1)S(1)}, bf16[1024,3072]{1,0:T(8,128)(2,1)}, u32[]{:S(2)}) copy-start(bf16[1024,3072]{1,0:T(8,128)(2,1)} %multiply_convert_fusion) | copy-start | bytes 18874372
  227.9 1.4 copy-start.4
  229.4 2.4 copy-start.5
  229.4 2.4 copy-start.9
  235.1 92.2 %copy-start.8 = (bf16[1024,768]{1,0:T(8,128)(2,1)S(1)}, bf16[1024,768]{1,0:T(8,128)(2,1)}, u32[]{:S(2)}) copy-start(bf16[1024,768]{1,0:T(8,128)(2,1)} %param.14) | copy-start | bytes 4718596
  327.3 7.9 %copy-start.13 = (f32[16,256]{1,0:T(8,128)S(1)}, f32[16,256]{1,0:T(8,128)}, u32[]{:S(2)}) copy-start(f32[16,256]{1,0:T(8,128)} %get-tuple-element.48) | copy-start | bytes 49156
  335.2 50.4 %copy-start.6 = (f32[1024,768]{0,1:T(8,128)S(1)}, f32[1024,768]{0,1:T(8,128)}, u32[]{:S(2)}) copy-start(f32[1024,768]{0,1:T(8,128)} %copy-done.5) | copy-start | bytes 9437188
  394.1 2.7 copy-start.2
  394.1 4.3 %copy-start.12 = (f32[48,384]{1,0:T(8,128)S(1)}, f32[48,384]{1,0:T(8,128)}, u32[]{:S(2)}) copy-start(f32[48,384]{1,0:T(8,128)} %get-tuple-element.50) | copy-start | bytes 221188
  394.1 4.9 %copy-start.11 = (f32[48,1536]{1,0:T(8,128)S(1)}, f32[48,1536]{1,0:T(8,128)}, u32[]{:S(2)}) copy-start(f32[48,1536]{1,0:T(8,128)} %get-tuple-element.140) | copy-start | bytes 884740
  394.1 5.7 %copy-start.10 = (f32[48,1536]{1,0:T(8,128)S(1)}, f32[48,1536]{1,0:T(8,128)}, u32[]{:S(2)}) copy-start(f32[48,1536]{1,0:T(8,128)} %get-tuple-element.52) | copy-start | bytes 884740
